TPU v7x, 256 devices: a whole 4x4x8 slice. The times are simulated.
256 devices in a mesh: dp: 2 (over core), expert: 128 (over z, x, y).
Axes of the slice: x: 4, y: 4, z: 8, core: 2. Of those that a mesh axis runs over, the one named last changes fastest.
Arguments:
- out_grad: bfloat16 [16384, 1024], P(('dp', 'expert')), may hold values from -6 to 6
- layer_input: bfloat16 [16384, 1024], P(('dp', 'expert')), may hold values from -6 to 6
- combine: float32 [16384, 8], P(('dp', 'expert')), may hold values from 0.05 to 0.5
- routes: int32 [16384, 8], P(('dp', 'expert')), may hold values from 0 to 127, all different within a row; in each aligned block of 64 rows (0 to 63, 64 to 127, ...) at most 8 rows name the same one
- w_gate_up: bfloat16 [128, 1024, 768], P('expert'), may hold values from -0.1875 to 0.1875
- w_down: bfloat16 [128, 384, 1024], P('expert'), may hold values from -0.3125 to 0.3125
- m_gate_up: float32 [128, 1024, 768], P('expert', 'dp'), may hold values from -0.75 to 0.75
- v_gate_up: float32 [128, 1024, 768], P('expert', 'dp'), may hold values from 0.001 to 0.1
- m_down: float32 [128, 384, 1024], P('expert', None, 'dp'), may hold values from -0.75 to 0.75
- v_down: float32 [128, 384, 1024], P('expert', None, 'dp'), may hold values from 0.001 to 0.1
- swap_pairs: int32 [32, 2], replicated, may hold values from 0 to 127, as said below
Outputs:
- in_grad: bfloat16 [16384, 1024], P(('dp', 'expert'))
- new_gate_up: bfloat16 [128, 1024, 768], P('expert', 'dp')
- new_down: bfloat16 [128, 384, 1024], P('expert', None, 'dp')
- new_m_gate_up: float32 [128, 1024, 768], P('expert', 'dp')
- new_v_gate_up: float32 [128, 1024, 768], P('expert', 'dp')
- new_m_down: float32 [128, 384, 1024], P('expert', None, 'dp')
- new_v_down: float32 [128, 384, 1024], P('expert', None, 'dp')
Inputs may be any that keep to these rules, and one draw needn't show every extreme that they name: `routes`: each row names 8 different experts; among the rows of one device no expert is named more than 8 times, a bound that some block reaches. `swap_pairs`: no device appears twice in the list; devices 0 and 127 are always in it.
All inputs are finite; a program needn't handle non-finite values. Where the computation divides by a largest or mean magnitude, that divisor is 1e-20 or more.
Results may differ from a plain program's by a relative error of at most 0.0064.
Values may be sent and summed in bfloat16 or wider, within the bound.
A program may use at most 128 MiB of HBM per device.

v0:
```python
import jax
import jax.numpy as jnp
from jax import lax
from jax.sharding import PartitionSpec as P

BETA_ONE = 0.9
BETA_TWO = 0.95
RATE = 0.001
DECAY = 0.1
ADAM_EPS = 1e-08
PEAK_EPS = 1e-06


def partner_table(swap_pairs, expert_count):
    devices = jnp.arange(expert_count, dtype=jnp.int32)
    first_dev = swap_pairs[:, 0]
    second_dev = swap_pairs[:, 1]
    hit_first = devices[:, None] == first_dev[None, :]
    hit_second = devices[:, None] == second_dev[None, :]
    other = jnp.sum(
        jnp.where(hit_first, second_dev[None, :], 0) + jnp.where(hit_second, first_dev[None, :], 0),
        axis=1,
    )
    paired = jnp.any(hit_first | hit_second, axis=1)
    return jnp.where(paired, other, devices)


def slot_ranks(route_ids, expert_count):
    flat_ids = route_ids.reshape(-1)
    onehot = (flat_ids[:, None] == jnp.arange(expert_count, dtype=jnp.int32)[None, :]).astype(
        jnp.int32
    )
    before = jnp.cumsum(onehot, axis=0) - onehot
    return jnp.sum(before * onehot, axis=1)


def expert_backward(slot_grad, slot_input, gate_up, down_proj):
    hidden_units = down_proj.shape[0]
    pre_act = jnp.dot(slot_input, gate_up, preferred_element_type=jnp.float32)
    gate_pre = pre_act[:, :hidden_units]
    up_pre = pre_act[:, hidden_units:]
    sigmoid_gate = jax.nn.sigmoid(gate_pre)
    gate_act = gate_pre * sigmoid_gate
    hidden = (gate_act * up_pre).astype(jnp.bfloat16)
    d_hidden = lax.dot_general(
        slot_grad, down_proj, (((1,), (1,)), ((), ())), preferred_element_type=jnp.float32
    )
    d_gate = d_hidden * up_pre * sigmoid_gate * (1.0 + gate_pre * (1.0 - sigmoid_gate))
    d_up = d_hidden * gate_act
    d_pre = jnp.concatenate([d_gate, d_up], axis=1).astype(jnp.bfloat16)
    grad_down = lax.dot_general(
        hidden, slot_grad, (((0,), (0,)), ((), ())), preferred_element_type=jnp.float32
    )
    grad_gate_up = lax.dot_general(
        slot_input, d_pre, (((0,), (0,)), ((), ())), preferred_element_type=jnp.float32
    )
    slot_back = lax.dot_general(
        d_pre, gate_up, (((1,), (1,)), ((), ())), preferred_element_type=jnp.float32
    ).astype(jnp.bfloat16)
    return (slot_back, grad_gate_up, grad_down)


def adam_update(weight, grad, mean_in, square_in, scale_by):
    scaled = grad * scale_by
    mean_new = BETA_ONE * mean_in + (1.0 - BETA_ONE) * scaled
    square_new = BETA_TWO * square_in + (1.0 - BETA_TWO) * scaled * scaled
    weight_wide = weight.astype(jnp.float32)
    step_size = mean_new / (jnp.sqrt(square_new) + ADAM_EPS)
    weight_new = (weight_wide - RATE * (step_size + DECAY * weight_wide)).astype(jnp.bfloat16)
    return (weight_new, mean_new, square_new)


def move_moments(gate_mean, gate_square, down_mean, down_square, partner):
    expert_count = partner.shape[0]
    spread_out = (
        lax.all_to_all(
            gate_mean.reshape(1, expert_count, -1),
            "expert",
            split_axis=1,
            concat_axis=0,
            tiled=True,
        ),
        lax.all_to_all(
            gate_square.reshape(1, expert_count, -1),
            "expert",
            split_axis=1,
            concat_axis=0,
            tiled=True,
        ),
        lax.all_to_all(
            down_mean.reshape(1, expert_count, -1),
            "expert",
            split_axis=1,
            concat_axis=0,
            tiled=True,
        ),
        lax.all_to_all(
            down_square.reshape(1, expert_count, -1),
            "expert",
            split_axis=1,
            concat_axis=0,
            tiled=True,
        ),
    )
    picked = [jnp.take(element, partner, axis=0) for element in spread_out]
    arrived = (
        lax.all_to_all(picked[0], "expert", split_axis=0, concat_axis=1, tiled=True),
        lax.all_to_all(picked[1], "expert", split_axis=0, concat_axis=1, tiled=True),
        lax.all_to_all(picked[2], "expert", split_axis=0, concat_axis=1, tiled=True),
        lax.all_to_all(picked[3], "expert", split_axis=0, concat_axis=1, tiled=True),
    )
    return (
        arrived[0].reshape(gate_mean.shape),
        arrived[1].reshape(gate_square.shape),
        arrived[2].reshape(down_mean.shape),
        arrived[3].reshape(down_square.shape),
    )


def move_weights_after(gate_up, down_proj, partner):
    expert_count = partner.shape[0]
    spread_out = (
        lax.all_to_all(
            gate_up.reshape(1, expert_count, -1), "expert", split_axis=1, concat_axis=0, tiled=True
        ),
        lax.all_to_all(
            down_proj.reshape(1, expert_count, -1),
            "expert",
            split_axis=1,
            concat_axis=0,
            tiled=True,
        ),
    )
    picked = [jnp.take(element, partner, axis=0) for element in spread_out]
    arrived = (
        lax.all_to_all(picked[0], "expert", split_axis=0, concat_axis=1, tiled=True),
        lax.all_to_all(picked[1], "expert", split_axis=0, concat_axis=1, tiled=True),
    )
    return (arrived[0].reshape(gate_up.shape), arrived[1].reshape(down_proj.shape))


def per_device(
    out_grad,
    layer_input,
    combine,
    routes,
    w_gate_up,
    w_down,
    m_gate_up,
    v_gate_up,
    m_down,
    v_down,
    swap_pairs,
):
    expert_count = lax.axis_size("expert")
    replicas = lax.axis_size("dp")
    replica = lax.axis_index("dp")
    partner = partner_table(swap_pairs, expert_count)
    tok_rows, top_count = routes.shape
    capacity = 2 * tok_rows * top_count // expert_count
    model_width = out_grad.shape[1]
    ranks = slot_ranks(routes, expert_count)
    assign = tok_rows * top_count
    slot_place = routes.reshape(-1) * capacity + ranks
    slot_owner = (
        jnp.full((expert_count * capacity,), -1, jnp.int32)
        .at[slot_place]
        .set(jnp.arange(assign, dtype=jnp.int32))
    )
    is_live = slot_owner >= 0
    safe_index = jnp.maximum(slot_owner, 0)
    token_ids = safe_index // top_count
    weights = jnp.where(is_live, combine.reshape(-1)[safe_index], jnp.float32(0.0))
    slot_grad = (out_grad[token_ids].astype(jnp.float32) * weights[:, None]).astype(jnp.bfloat16)
    slot_input = jnp.where(is_live[:, None], layer_input[token_ids], jnp.zeros((), jnp.bfloat16))
    slot_grad, slot_input = (
        lax.all_to_all(
            slot_grad.reshape(expert_count, capacity, model_width),
            "expert",
            split_axis=0,
            concat_axis=0,
            tiled=True,
        ),
        lax.all_to_all(
            slot_input.reshape(expert_count, capacity, model_width),
            "expert",
            split_axis=0,
            concat_axis=0,
            tiled=True,
        ),
    )
    slot_back, grad_gate_up, grad_down = expert_backward(
        slot_grad.reshape(-1, model_width),
        slot_input.reshape(-1, model_width),
        w_gate_up[0],
        w_down[0],
    )
    slot_back = lax.all_to_all(
        slot_back.reshape(expert_count, capacity, model_width),
        "expert",
        split_axis=0,
        concat_axis=0,
        tiled=True,
    )
    returned = slot_back.reshape(expert_count * capacity, model_width)[slot_place].reshape(
        tok_rows, top_count, model_width
    )
    in_grad = jnp.sum(returned, axis=1, dtype=jnp.float32).astype(jnp.bfloat16)
    half_rows = model_width // replicas
    part_gate_up, part_down = (
        lax.psum_scatter(
            grad_gate_up.astype(jnp.bfloat16), "dp", scatter_dimension=0, tiled=True
        ).astype(jnp.float32),
        lax.psum_scatter(
            grad_down.astype(jnp.bfloat16), "dp", scatter_dimension=1, tiled=True
        ).astype(jnp.float32),
    )
    local_peak = jnp.maximum(jnp.max(jnp.abs(part_gate_up)), jnp.max(jnp.abs(part_down)))
    peak_abs = lax.pmax(local_peak, "dp")
    scale_by = 1.0 / (peak_abs + PEAK_EPS)
    own_gate_up = lax.dynamic_slice_in_dim(w_gate_up[0], replica * half_rows, half_rows, 0)
    own_down = lax.dynamic_slice_in_dim(w_down[0], replica * half_rows, half_rows, 1)
    new_gu, gate_mean, gate_square = adam_update(
        own_gate_up, part_gate_up, m_gate_up[0], v_gate_up[0], scale_by
    )
    new_dn, down_mean, down_square = adam_update(
        own_down, part_down, m_down[0], v_down[0], scale_by
    )
    new_gu, new_dn = move_weights_after(new_gu, new_dn, partner)
    gate_mean, gate_square, down_mean, down_square = move_moments(
        gate_mean, gate_square, down_mean, down_square, partner
    )
    return (
        in_grad,
        new_gu[None],
        new_dn[None],
        gate_mean[None],
        gate_square[None],
        down_mean[None],
        down_square[None],
    )


def solution(mesh):
    in_specs = (
        P(("dp", "expert"), None),
        P(("dp", "expert"), None),
        P(("dp", "expert"), None),
        P(("dp", "expert"), None),
        P("expert", None, None),
        P("expert", None, None),
        P("expert", "dp", None),
        P("expert", "dp", None),
        P("expert", None, "dp"),
        P("expert", None, "dp"),
        P(),
    )
    out_specs = (
        P(("dp", "expert"), None),
        P("expert", "dp", None),
        P("expert", None, "dp"),
        P("expert", "dp", None),
        P("expert", "dp", None),
        P("expert", None, "dp"),
        P("expert", None, "dp"),
    )
    return jax.shard_map(
        per_device, mesh=mesh, in_specs=in_specs, out_specs=out_specs, check_vma=False
    )
```

profile of v0, /device:TPU:2, one launch (start us, length us, event | category | flops | bytes accessed | tf_op | source)
XLA Modules:
  0.0 669.4 jit_solution(3657734862248697985)
XLA Ops:
  13.1 6.9 %gather_fusion.1 = f32[1024]{0:T(1024)S(1)} fusion(f32[512]{0:T(512)S(1)} %reshape.312, s32[1024]{0:T(1024)S(1)} %get-tuple-element.21), kind=kCustom, calls=%fused_computation.5 | custom fusion | bytes 12288 | tf_op jit(solution)/shard_map/gather | solution.py:173
  20.1 4.1 gather_fusion.2
  25.7 16.0 %all-to-all-start.1 = ((bf16[128,8,1024]{2,1,0:T(8,128)(2,1)}), bf16[128,8,1024]{2,1,0:T(8,128)(2,1)}, u32[]{:S(2)}, u32[]{:S(2)}) async-start(bf16[128,8,1024]{2,1,0:T(8,128)(2,1)} %bitcast_select_fusion), calls=%async_computation.1 | async-start | bytes 4194304 | tf_op jit(solution)/shard_map/all_to_all | solution.py:184
  41.8 4.1 gather_fusion
  47.7 46.3 %all-to-all-done.1 = bf16[128,8,1024]{2,1,0:T(8,128)(2,1)} async-done(((bf16[128,8,1024]{2,1,0:T(8,128)(2,1)}), bf16[128,8,1024]{2,1,0:T(8,128)(2,1)}, u32[]{:S(2)}, u32[]{:S(2)}) %all-to-all-start.1) | async-done | bytes 2097184 | tf_op jit(solution)/shard_map/all_to_all | solution.py:184
  94.0 7.2 %all-to-all-start = ((bf16[128,8,1024]{2,1,0:T(8,128)(2,1)}), bf16[128,8,1024]{2,1,0:T(8,128)(2,1)S(1)}, u32[]{:S(2)}, u32[]{:S(2)}) async-start(bf16[128,8,1024]{2,1,0:T(8,128)(2,1)} %fusion), calls=%async_computation | async-start | bytes 4194304 | tf_op jit(solution)/shard_map/all_to_all | solution.py:177
  101.3 5.5 fusion.3
  106.9 46.3 %all-to-all-done = bf16[128,8,1024]{2,1,0:T(8,128)(2,1)S(1)} async-done(((bf16[128,8,1024]{2,1,0:T(8,128)(2,1)}), bf16[128,8,1024]{2,1,0:T(8,128)(2,1)S(1)}, u32[]{:S(2)}, u32[]{:S(2)}) %all-to-all-start) | async-done | bytes 2097184 | tf_op jit(solution)/shard_map/all_to_all | solution.py:177
  153.1 3.8 fusion.22
  157.2 3.3 multiply_convert_fusion.2
  161.6 4.6 fusion.10
  168.1 16.2 %reduce-scatter.3.cloned.1.call-done = bf16[512,768]{1,0:T(8,128)(2,1)} async-done(((bf16[1024,768]{1,0:T(8,128)(2,1)}), bf16[512,768]{1,0:T(8,128)(2,1)}) %reduce-scatter.3.cloned.1.call-update) | async-done | bytes 786448 | tf_op jit(solution)/shard_map/reduce_scatter | solution.py:211
  198.4 13.8 %all-to-all-start.5 = ((bf16[128,2,768]{2,1,0:T(2,128)(2,1)}), bf16[128,2,768]{2,1,0:T(2,128)(2,1)S(1)}, u32[]{:S(2)}, u32[]{:S(2)}) async-start(bf16[128,2,768]{2,1,0:T(2,128)(2,1)} %reshape.474), calls=%async_computation.7 | async-start | bytes 786432 | tf_op jit(solution)/shard_map/all_to_all | solution.py:126
  212.2 4.9 convert_bitcast_fusion
  217.0 12.9 %all-to-all-done.5 = bf16[128,2,768]{2,1,0:T(2,128)(2,1)S(1)} async-done(((bf16[128,2,768]{2,1,0:T(2,128)(2,1)}), bf16[128,2,768]{2,1,0:T(2,128)(2,1)S(1)}, u32[]{:S(2)}, u32[]{:S(2)}) %all-to-all-start.5) | async-done | bytes 393248 | tf_op jit(solution)/shard_map/all_to_all | solution.py:126
  230.7 7.1 %all-to-all-start.2 = ((bf16[128,8,1024]{2,1,0:T(8,128)(2,1)}), bf16[128,8,1024]{2,1,0:T(8,128)(2,1)S(1)}, u32[]{:S(2)}, u32[]{:S(2)}) async-start(bf16[128,8,1024]{2,1,0:T(8,128)(2,1)} %convert_bitcast_fusion), calls=%async_computation.2 | async-start | bytes 4194304 | tf_op jit(solution)/shard_map/all_to_all | solution.py:198
  240.8 48.4 %all-to-all-done.2 = bf16[128,8,1024]{2,1,0:T(8,128)(2,1)S(1)} async-done(((bf16[128,8,1024]{2,1,0:T(8,128)(2,1)}), bf16[128,8,1024]{2,1,0:T(8,128)(2,1)S(1)}, u32[]{:S(2)}, u32[]{:S(2)}) %all-to-all-start.2) | async-done | bytes 2097184 | tf_op jit(solution)/shard_map/all_to_all | solution.py:198
  289.1 7.5 %all-to-all-start.13 = ((f32[1,128,1536]{2,0,1:T(1,128)}), f32[1,128,1536]{2,0,1:T(1,128)}, u32[]{:S(2)}, u32[]{:S(2)}) async-start(f32[1,128,1536]{2,0,1:T(1,128)} %reshape.460), calls=%async_computation.15 | async-start | bytes 1572864 | tf_op jit(solution)/shard_map/all_to_all | solution.py:97
  298.5 21.6 %all-to-all-done.13 = f32[1,128,1536]{2,0,1:T(1,128)} async-done(((f32[1,128,1536]{2,0,1:T(1,128)}), f32[1,128,1536]{2,0,1:T(1,128)}, u32[]{:S(2)}, u32[]{:S(2)}) %all-to-all-start.13) | async-done | bytes 786464 | tf_op jit(solution)/shard_map/all_to_all | solution.py:97
  320.0 8.0 %all-to-all-start.11 = ((f32[1,128,1536]{2,0,1:T(1,128)}), f32[1,128,1536]{2,0,1:T(1,128)}, u32[]{:S(2)}, u32[]{:S(2)}) async-start(f32[1,128,1536]{2,0,1:T(1,128)} %reshape.458), calls=%async_computation.13 | async-start | bytes 1572864 | tf_op jit(solution)/shard_map/all_to_all | solution.py:90
  328.1 4.8 fusion.17
  332.8 4.5 reshape.452
  337.4 6.2 reduce.7
  343.6 3.3 reshape.470
  346.9 3.3 all-to-all-done.11
  350.2 10.9 %all-to-all-start.3 = ((bf16[128,2,1536]{2,1,0:T(2,128)(2,1)}), bf16[128,2,1536]{2,1,0:T(2,128)(2,1)}, u32[]{:S(2)}, u32[]{:S(2)}) async-start(bf16[128,2,1536]{2,1,0:T(2,128)(2,1)} %reshape.470), calls=%async_computation.5 | async-start | bytes 1572864 | tf_op jit(solution)/shard_map/all_to_all | solution.py:123
  364.6 18.3 %all-to-all-done.3 = bf16[128,2,1536]{2,1,0:T(2,128)(2,1)} async-done(((bf16[128,2,1536]{2,1,0:T(2,128)(2,1)}), bf16[128,2,1536]{2,1,0:T(2,128)(2,1)}, u32[]{:S(2)}, u32[]{:S(2)}) %all-to-all-start.3) | async-done | bytes 786464 | tf_op jit(solution)/shard_map/all_to_all | solution.py:123
  382.8 7.9 %all-to-all-start.6 = ((bf16[128,2,768]{2,1,0:T(2,128)(2,1)}), bf16[128,2,768]{2,1,0:T(2,128)(2,1)}, u32[]{:S(2)}, u32[]{:S(2)}) async-start(bf16[128,2,768]{2,1,0:T(2,128)(2,1)} %reshape.476), calls=%async_computation.8 | async-start | bytes 786432 | tf_op jit(solution)/shard_map/all_to_all | solution.py:137
  399.7 5.4 all-to-all-done.6
  405.1 8.8 %all-to-all-start.14 = ((f32[128,1,1536]{2,1,0:T(1,128)}), f32[128,1,1536]{2,1,0:T(1,128)}, u32[]{:S(2)}, u32[]{:S(2)}) async-start(f32[128,1,1536]{2,1,0:T(1,128)} %copy.77), calls=%async_computation.16 | async-start | bytes 1572864 | tf_op jit(solution)/shard_map/all_to_all | solution.py:110
  416.9 16.9 %all-to-all-done.14 = f32[128,1,1536]{2,1,0:T(1,128)} async-done(((f32[128,1,1536]{2,1,0:T(1,128)}), f32[128,1,1536]{2,1,0:T(1,128)}, u32[]{:S(2)}, u32[]{:S(2)}) %all-to-all-start.14) | async-done | bytes 786464 | tf_op jit(solution)/shard_map/all_to_all | solution.py:110
  433.8 7.7 %all-to-all-start.12 = ((f32[128,1,1536]{2,1,0:T(1,128)}), f32[128,1,1536]{2,1,0:T(1,128)}, u32[]{:S(2)}, u32[]{:S(2)}) async-start(f32[128,1,1536]{2,1,0:T(1,128)} %copy.75), calls=%async_computation.14 | async-start | bytes 1572864 | tf_op jit(solution)/shard_map/all_to_all | solution.py:109
  444.2 16.0 %all-to-all-done.12 = f32[128,1,1536]{2,1,0:T(1,128)} async-done(((f32[128,1,1536]{2,1,0:T(1,128)}), f32[128,1,1536]{2,1,0:T(1,128)}, u32[]{:S(2)}, u32[]{:S(2)}) %all-to-all-start.12) | async-done | bytes 786464 | tf_op jit(solution)/shard_map/all_to_all | solution.py:109
  460.2 7.3 %all-to-all-start.9 = ((f32[1,128,3072]{2,0,1:T(1,128)}), f32[1,128,3072]{2,0,1:T(1,128)S(1)}, u32[]{:S(2)}, u32[]{:S(2)}) async-start(f32[1,128,3072]{2,0,1:T(1,128)} %reshape.456), calls=%async_computation.11 | async-start | bytes 3145728 | tf_op jit(solution)/shard_map/all_to_all | solution.py:83
  470.2 31.2 %all-to-all-done.9 = f32[1,128,3072]{2,0,1:T(1,128)S(1)} async-done(((f32[1,128,3072]{2,0,1:T(1,128)}), f32[1,128,3072]{2,0,1:T(1,128)S(1)}, u32[]{:S(2)}, u32[]{:S(2)}) %all-to-all-start.9) | async-done | bytes 1572896 | tf_op jit(solution)/shard_map/all_to_all | solution.py:83
  501.4 7.5 %all-to-all-start.7 = ((f32[1,128,3072]{2,0,1:T(1,128)}), f32[1,128,3072]{2,0,1:T(1,128)}, u32[]{:S(2)}, u32[]{:S(2)}) async-start(f32[1,128,3072]{2,0,1:T(1,128)} %reshape.454), calls=%async_computation.9 | async-start | bytes 3145728 | tf_op jit(solution)/shard_map/all_to_all | solution.py:76
  508.9 6.0 reshape.471
  520.3 23.0 %all-to-all-done.7 = f32[1,128,3072]{2,0,1:T(1,128)} async-done(((f32[1,128,3072]{2,0,1:T(1,128)}), f32[1,128,3072]{2,0,1:T(1,128)}, u32[]{:S(2)}, u32[]{:S(2)}) %all-to-all-start.7) | async-done | bytes 1572896 | tf_op jit(solution)/shard_map/all_to_all | solution.py:76
  543.4 7.5 %all-to-all-start.4 = ((bf16[128,2,1536]{2,1,0:T(2,128)(2,1)}), bf16[128,2,1536]{2,1,0:T(2,128)(2,1)}, u32[]{:S(2)}, u32[]{:S(2)}) async-start(bf16[128,2,1536]{2,1,0:T(2,128)(2,1)} %reshape.472), calls=%async_computation.6 | async-start | bytes 1572864 | tf_op jit(solution)/shard_map/all_to_all | solution.py:136
  560.9 9.3 %all-to-all-done.4 = bf16[128,2,1536]{2,1,0:T(2,128)(2,1)} async-done(((bf16[128,2,1536]{2,1,0:T(2,128)(2,1)}), bf16[128,2,1536]{2,1,0:T(2,128)(2,1)}, u32[]{:S(2)}, u32[]{:S(2)}) %all-to-all-start.4) | async-done | bytes 786464 | tf_op jit(solution)/shard_map/all_to_all | solution.py:136
  570.2 7.9 %all-to-all-start.10 = ((f32[128,1,3072]{2,1,0:T(1,128)}), f32[128,1,3072]{2,1,0:T(1,128)}, u32[]{:S(2)}, u32[]{:S(2)}) async-start(f32[128,1,3072]{2,1,0:T(1,128)} %copy.73), calls=%async_computation.12 | async-start | bytes 3145728 | tf_op jit(solution)/shard_map/all_to_all | solution.py:108
  580.8 31.5 %all-to-all-done.10 = f32[128,1,3072]{2,1,0:T(1,128)} async-done(((f32[128,1,3072]{2,1,0:T(1,128)}), f32[128,1,3072]{2,1,0:T(1,128)}, u32[]{:S(2)}, u32[]{:S(2)}) %all-to-all-start.10) | async-done | bytes 1572896 | tf_op jit(solution)/shard_map/all_to_all | solution.py:108
  612.3 7.5 %all-to-all-start.8 = ((f32[128,1,3072]{2,1,0:T(1,128)}), f32[128,1,3072]{2,1,0:T(1,128)}, u32[]{:S(2)}, u32[]{:S(2)}) async-start(f32[128,1,3072]{2,1,0:T(1,128)} %copy.71), calls=%async_computation.10 | async-start | bytes 3145728 | tf_op jit(solution)/shard_map/all_to_all | solution.py:107
  629.3 3.0 reduce.6
  637.4 5.3 reshape.473
  642.7 4.7 reduce.1
  648.7 5.1 reduce.4
  655.5 5.1 reduce.3
  (120 shorter events, 88.0 us)
Async XLA Ops:
  7.2 12.9 %copy-start = (bf16[64,1024]{1,0:T(8,128)(2,1)S(1)}, bf16[64,1024]{1,0:T(8,128)(2,1)}, u32[]{:S(2)}) copy-start(bf16[64,1024]{1,0:T(8,128)(2,1)} %param.16) | copy-start | bytes 393220
  25.7 16.1 %copy-start.2 = (bf16[64,1024]{1,0:T(8,128)(2,1)S(1)}, bf16[64,1024]{1,0:T(8,128)(2,1)}, u32[]{:S(2)}) copy-start(bf16[64,1024]{1,0:T(8,128)(2,1)} %param.15) | copy-start | bytes 393220
  25.7 68.3 %all-to-all-start.1 = ((bf16[128,8,1024]{2,1,0:T(8,128)(2,1)}), bf16[128,8,1024]{2,1,0:T(8,128)(2,1)}, u32[]{:S(2)}, u32[]{:S(2)}) async-start(bf16[128,8,1024]{2,1,0:T(8,128)(2,1)} %bitcast_select_fusion), calls=%async_computation.1 | async-start | bytes 4194304 | tf_op jit(solution)/shard_map/all_to_all | solution.py:184
  94.0 59.1 %all-to-all-start = ((bf16[128,8,1024]{2,1,0:T(8,128)(2,1)}), bf16[128,8,1024]{2,1,0:T(8,128)(2,1)S(1)}, u32[]{:S(2)}, u32[]{:S(2)}) async-start(bf16[128,8,1024]{2,1,0:T(8,128)(2,1)} %fusion), calls=%async_computation | async-start | bytes 4194304 | tf_op jit(solution)/shard_map/all_to_all | solution.py:177
  101.3 65.1 %reduce-scatter.5.cloned.1.call-start = ((), (), s32[]{:S(2)}) async-start(), calls=%async_computation.18 | async-start | bytes 1179648 | tf_op jit(solution)/shard_map/reduce_scatter | solution.py:214
  106.9 50.3 %copy-start.11 = (bf16[1,384,1024]{2,1,0:T(8,128)(2,1)S(1)}, bf16[1,384,1024]{2,1,0:T(8,128)(2,1)}, u32[]{:S(2)}) copy-start(bf16[1,384,1024]{2,1,0:T(8,128)(2,1)} %param.20) | copy-start | bytes 2359300
  156.9 27.4 %reduce-scatter.3.cloned.1.call-start = ((), (), s32[]{:S(2)}) async-start(), calls=%async_computation.17 | async-start | bytes 2359296 | tf_op jit(solution)/shard_map/reduce_scatter | solution.py:211
  160.5 0.9 copy-start.13
  160.5 1.1 copy-start.15
  166.3 24.9 %copy-start.9 = (f32[1,384,512]{2,1,0:T(8,128)S(1)}, f32[1,384,512]{2,1,0:T(8,128)}, u32[]{:S(2)}) copy-start(f32[1,384,512]{2,1,0:T(8,128)} %param.24) | copy-start | bytes 2359300
  166.3 24.9 %copy-start.10 = (f32[1,384,512]{2,1,0:T(8,128)S(1)}, f32[1,384,512]{2,1,0:T(8,128)}, u32[]{:S(2)}) copy-start(f32[1,384,512]{2,1,0:T(8,128)} %param.23) | copy-start | bytes 2359300
  194.0 18.1 %copy-start.14 = (bf16[1024,384]{0,1:T(8,128)(2,1)S(1)}, bf16[1024,384]{0,1:T(8,128)(2,1)}, u32[]{:S(2)}) copy-start(bf16[1024,384]{0,1:T(8,128)(2,1)} %copy-done.13) | copy-start | bytes 2359300
  198.4 31.6 %all-to-all-start.5 = ((bf16[128,2,768]{2,1,0:T(2,128)(2,1)}), bf16[128,2,768]{2,1,0:T(2,128)(2,1)S(1)}, u32[]{:S(2)}, u32[]{:S(2)}) async-start(bf16[128,2,768]{2,1,0:T(2,128)(2,1)} %reshape.474), calls=%async_computation.7 | async-start | bytes 786432 | tf_op jit(solution)/shard_map/all_to_all | solution.py:126
  230.0 0.7 copy-start.7
  230.7 58.4 %all-to-all-start.2 = ((bf16[128,8,1024]{2,1,0:T(8,128)(2,1)}), bf16[128,8,1024]{2,1,0:T(8,128)(2,1)S(1)}, u32[]{:S(2)}, u32[]{:S(2)}) async-start(bf16[128,8,1024]{2,1,0:T(8,128)(2,1)} %convert_bitcast_fusion), calls=%async_computation.2 | async-start | bytes 4194304 | tf_op jit(solution)/shard_map/all_to_all | solution.py:198
  289.1 9.3 %copy-start.3 = (bf16[128,8,1024]{2,1,0:T(8,128)(2,1)}, bf16[128,8,1024]{2,1,0:T(8,128)(2,1)S(1)}, u32[]{:S(2)}) copy-start(bf16[128,8,1024]{2,1,0:T(8,128)(2,1)S(1)} %all-to-all-done.2) | copy-start | bytes 6291460
  289.1 30.9 %all-to-all-start.13 = ((f32[1,128,1536]{2,0,1:T(1,128)}), f32[1,128,1536]{2,0,1:T(1,128)}, u32[]{:S(2)}, u32[]{:S(2)}) async-start(f32[1,128,1536]{2,0,1:T(1,128)} %reshape.460), calls=%async_computation.15 | async-start | bytes 1572864 | tf_op jit(solution)/shard_map/all_to_all | solution.py:97
  298.5 29.6 %copy-start.6 = (bf16[512,768]{1,0:T(8,128)(2,1)S(1)}, bf16[512,768]{1,0:T(8,128)(2,1)}, u32[]{:S(2)}) copy-start(bf16[512,768]{1,0:T(8,128)(2,1)} %reduce-scatter.3.cloned.1.call-done) | copy-start | bytes 2359300
  320.0 30.2 %all-to-all-start.11 = ((f32[1,128,1536]{2,0,1:T(1,128)}), f32[1,128,1536]{2,0,1:T(1,128)}, u32[]{:S(2)}, u32[]{:S(2)}) async-start(f32[1,128,1536]{2,0,1:T(1,128)} %reshape.458), calls=%async_computation.13 | async-start | bytes 1572864 | tf_op jit(solution)/shard_map/all_to_all | solution.py:90
  343.6 17.6 %copy-start.12 = (s32[32,2]{0,1:T(2,128)S(1)}, s32[32,2]{0,1:T(2,128)}, u32[]{:S(2)}) copy-start(s32[32,2]{0,1:T(2,128)} %param.25) | copy-start | bytes 772
  343.6 17.8 %copy-start.8 = (bf16[128,2,768]{2,1,0:T(2,128)(2,1)S(1)}, bf16[128,2,768]{2,1,0:T(2,128)(2,1)}, u32[]{:S(2)}) copy-start(bf16[128,2,768]{2,1,0:T(2,128)(2,1)} %copy-done.7) | copy-start | bytes 1179652
  350.2 32.6 %all-to-all-start.3 = ((bf16[128,2,1536]{2,1,0:T(2,128)(2,1)}), bf16[128,2,1536]{2,1,0:T(2,128)(2,1)}, u32[]{:S(2)}, u32[]{:S(2)}) async-start(bf16[128,2,1536]{2,1,0:T(2,128)(2,1)} %reshape.470), calls=%async_computation.5 | async-start | bytes 1572864 | tf_op jit(solution)/shard_map/all_to_all | solution.py:123
  382.8 22.2 %all-to-all-start.6 = ((bf16[128,2,768]{2,1,0:T(2,128)(2,1)}), bf16[128,2,768]{2,1,0:T(2,128)(2,1)}, u32[]{:S(2)}, u32[]{:S(2)}) async-start(bf16[128,2,768]{2,1,0:T(2,128)(2,1)} %reshape.476), calls=%async_computation.8 | async-start | bytes 786432 | tf_op jit(solution)/shard_map/all_to_all | solution.py:137
  405.1 28.7 %all-to-all-start.14 = ((f32[128,1,1536]{2,1,0:T(1,128)}), f32[128,1,1536]{2,1,0:T(1,128)}, u32[]{:S(2)}, u32[]{:S(2)}) async-start(f32[128,1,1536]{2,1,0:T(1,128)} %copy.77), calls=%async_computation.16 | async-start | bytes 1572864 | tf_op jit(solution)/shard_map/all_to_all | solution.py:110
  413.9 27.6 %copy-start.5 = (f32[512,768]{1,0:T(8,128)S(1)}, f32[512,768]{1,0:T(8,128)}, u32[]{:S(2)}) copy-start(f32[512,768]{1,0:T(8,128)} %get-tuple-element.15) | copy-start | bytes 4718596
  433.8 26.4 %all-to-all-start.12 = ((f32[128,1,1536]{2,1,0:T(1,128)}), f32[128,1,1536]{2,1,0:T(1,128)}, u32[]{:S(2)}, u32[]{:S(2)}) async-start(f32[128,1,1536]{2,1,0:T(1,128)} %copy.75), calls=%async_computation.14 | async-start | bytes 1572864 | tf_op jit(solution)/shard_map/all_to_all | solution.py:109
  460.2 41.2 %all-to-all-start.9 = ((f32[1,128,3072]{2,0,1:T(1,128)}), f32[1,128,3072]{2,0,1:T(1,128)S(1)}, u32[]{:S(2)}, u32[]{:S(2)}) async-start(f32[1,128,3072]{2,0,1:T(1,128)} %reshape.456), calls=%async_computation.11 | async-start | bytes 3145728 | tf_op jit(solution)/shard_map/all_to_all | solution.py:83
  501.4 42.0 %all-to-all-start.7 = ((f32[1,128,3072]{2,0,1:T(1,128)}), f32[1,128,3072]{2,0,1:T(1,128)}, u32[]{:S(2)}, u32[]{:S(2)}) async-start(f32[1,128,3072]{2,0,1:T(1,128)} %reshape.454), calls=%async_computation.9 | async-start | bytes 3145728 | tf_op jit(solution)/shard_map/all_to_all | solution.py:76
  543.4 26.8 %all-to-all-start.4 = ((bf16[128,2,1536]{2,1,0:T(2,128)(2,1)}), bf16[128,2,1536]{2,1,0:T(2,128)(2,1)}, u32[]{:S(2)}, u32[]{:S(2)}) async-start(bf16[128,2,1536]{2,1,0:T(2,128)(2,1)} %reshape.472), calls=%async_computation.6 | async-start | bytes 1572864 | tf_op jit(solution)/shard_map/all_to_all | solution.py:136
  570.2 42.1 %all-to-all-start.10 = ((f32[128,1,3072]{2,1,0:T(1,128)}), f32[128,1,3072]{2,1,0:T(1,128)}, u32[]{:S(2)}, u32[]{:S(2)}) async-start(f32[128,1,3072]{2,1,0:T(1,128)} %copy.73), calls=%async_computation.12 | async-start | bytes 3145728 | tf_op jit(solution)/shard_map/all_to_all | solution.py:108
  580.8 39.0 %copy-start.4 = (bf16[128,8,1024]{2,1,0:T(8,128)(2,1)S(1)}, bf16[128,8,1024]{2,1,0:T(8,128)(2,1)}, u32[]{:S(2)}) copy-start(bf16[128,8,1024]{2,1,0:T(8,128)(2,1)} %copy-done.3) | copy-start | bytes 6291460
  612.3 43.1 %all-to-all-start.8 = ((f32[128,1,3072]{2,1,0:T(1,128)}), f32[128,1,3072]{2,1,0:T(1,128)}, u32[]{:S(2)}, u32[]{:S(2)}) async-start(f32[128,1,3072]{2,1,0:T(1,128)} %copy.71), calls=%async_computation.10 | async-start | bytes 3145728 | tf_op jit(solution)/shard_map/all_to_all | solution.py:107
  655.5 6.7 %copy-start.1 = (bf16[64,1024]{1,0:T(8,128)(2,1)S(1)}, bf16[64,1024]{1,0:T(8,128)(2,1)}, u32[]{:S(2)}) copy-start(bf16[64,1024]{1,0:T(8,128)(2,1)} %param.16) | copy-start | bytes 393220
Sparse Core Ops, SparseCore 0:
  157.1 8.2 reduce-scatter.4
  168.6 15.7 reduce-scatter.2
where the time goes:
time: 679 us; the launch traced here: 669 us
  waiting for transfers between devices  347 us (51%)
  starting transfers between devices  133 us (20%)
  local copies, waits for them, and re-layouts  91.6 us (13%)
  other arithmetic  56.2 us (8%)
  matrix products  22.1 us (3%)
  between operations  17 us (3%)
    all_to_all x1, waiting for transfers between devices, per_device(): lax.all_to_all(slot_back.reshape(expert_count, capacity, model_width), 'e...  48.4 us
    all_to_all x1, waiting for transfers between devices, per_device(): lax.all_to_all(slot_input.reshape(expert_count, capacity, model_width), '...  46.3 us
    all_to_all x1, waiting for transfers between devices, per_device(): lax.all_to_all(slot_grad.reshape(expert_count, capacity, model_width), 'e...  46.3 us
    all_to_all x1, waiting for transfers between devices, move_moments(): lax.all_to_all(picked[1], 'expert', split_axis=0, concat_axis=1, tiled=True)  31.5 us
    all_to_all x1, waiting for transfers between devices, move_moments(): lax.all_to_all(gate_square.reshape(1, expert_count, -1), 'expert', split_...  31.2 us
    unnamed x50, local copies, waits for them, and re-layouts  30.7 us
    all_to_all x1, waiting for transfers between devices, move_moments(): lax.all_to_all(gate_mean.reshape(1, expert_count, -1), 'expert', split_ax...  23 us
    all_to_all x1, waiting for transfers between devices, move_moments(): lax.all_to_all(down_square.reshape(1, expert_count, -1), 'expert', split_...  21.6 us
  transfers between devices with their start and end apart: 17, of which 15 were waited for; matrix products, arithmetic and copies ran while one was open for 19% of the time, Pallas kernels for 0%

commit v1 on v0

v1 whole, which is shorter than its diff:
```python
import jax
import jax.numpy as jnp
from jax import lax
from jax.sharding import PartitionSpec as P

BETA_ONE = 0.9
BETA_TWO = 0.95
RATE = 0.001
DECAY = 0.1
ADAM_EPS = 1e-08
PEAK_EPS = 1e-06
SUB = 8
LANE = 128


def partner_table(swap_pairs, expert_count):
    devices = jnp.arange(expert_count, dtype=jnp.int32)
    first_dev = swap_pairs[:, 0]
    second_dev = swap_pairs[:, 1]
    hit_first = devices[:, None] == first_dev[None, :]
    hit_second = devices[:, None] == second_dev[None, :]
    other = jnp.sum(
        jnp.where(hit_first, second_dev[None, :], 0) + jnp.where(hit_second, first_dev[None, :], 0),
        axis=1,
    )
    paired = jnp.any(hit_first | hit_second, axis=1)
    return jnp.where(paired, other, devices)


def slot_select(routes, combine, expert_count, capacity):
    tok_rows = routes.shape[0]
    experts = jnp.arange(expert_count, dtype=jnp.int32)
    hit = routes[:, :, None] == experts[None, None, :]
    member = jnp.any(hit, axis=1)
    weight = jnp.sum(jnp.where(hit, combine[:, :, None], jnp.float32(0.0)), axis=1)
    earlier = jnp.tril(jnp.ones((tok_rows, tok_rows), jnp.bfloat16), -1)
    rank = jnp.dot(earlier, member.astype(jnp.bfloat16), preferred_element_type=jnp.float32)
    place = jnp.where(member, rank.astype(jnp.int32), -1)
    slots = jnp.arange(capacity, dtype=jnp.int32)
    chosen = place.T[:, None, :] == slots[None, :, None]
    slot_weight = jnp.sum(jnp.where(chosen, weight.T[:, None, :], jnp.float32(0.0)), axis=2)
    select = chosen.astype(jnp.bfloat16).reshape(expert_count * capacity, tok_rows)
    return select, slot_weight.reshape(expert_count * capacity)


def to_tiles(matrix):
    rows, cols = matrix.shape
    tiles = matrix.reshape(rows // SUB, SUB, cols // LANE, LANE).transpose(0, 2, 1, 3)
    return tiles.reshape(-1, SUB, LANE)


def from_tiles(tiles, rows, cols):
    return (
        tiles.reshape(rows // SUB, cols // LANE, SUB, LANE).transpose(0, 2, 1, 3).reshape(rows, cols)
    )


def adam_update(weight, grad, mean_in, square_in, scale_by):
    scaled = grad * scale_by
    mean_new = BETA_ONE * mean_in + (1.0 - BETA_ONE) * scaled
    square_new = BETA_TWO * square_in + (1.0 - BETA_TWO) * scaled * scaled
    weight_wide = weight.astype(jnp.float32)
    step_size = mean_new / (jnp.sqrt(square_new) + ADAM_EPS)
    weight_new = weight_wide - RATE * (step_size + DECAY * weight_wide)
    return (
        weight_new.astype(jnp.bfloat16),
        mean_new.astype(jnp.bfloat16),
        square_new.astype(jnp.bfloat16),
    )


def per_device(
    out_grad,
    layer_input,
    combine,
    routes,
    w_gate_up,
    w_down,
    m_gate_up,
    v_gate_up,
    m_down,
    v_down,
    swap_pairs,
):
    expert_count = lax.axis_size("expert")
    replicas = lax.axis_size("dp")
    replica = lax.axis_index("dp")
    partner = partner_table(swap_pairs, expert_count)
    tok_rows, top_count = routes.shape
    capacity = 2 * tok_rows * top_count // expert_count
    model_width = out_grad.shape[1]
    gate_up = w_gate_up[0]
    down_proj = w_down[0]
    hidden_units = down_proj.shape[0]

    def swap_tokens(rows):
        return lax.all_to_all(
            rows.reshape(expert_count, capacity, model_width),
            "expert",
            split_axis=0,
            concat_axis=0,
            tiled=True,
        ).reshape(expert_count * capacity, model_width)

    select, slot_weight = slot_select(routes, combine, expert_count, capacity)
    slot_input = jnp.dot(select, layer_input, preferred_element_type=jnp.float32).astype(
        jnp.bfloat16
    )
    slot_input = swap_tokens(slot_input)
    slot_grad = (
        jnp.dot(select, out_grad, preferred_element_type=jnp.float32) * slot_weight[:, None]
    ).astype(jnp.bfloat16)
    slot_grad = swap_tokens(slot_grad)

    pre_act = jnp.dot(slot_input, gate_up, preferred_element_type=jnp.float32)
    gate_pre = pre_act[:, :hidden_units]
    up_pre = pre_act[:, hidden_units:]
    sigmoid_gate = jax.nn.sigmoid(gate_pre)
    gate_act = gate_pre * sigmoid_gate
    hidden = (gate_act * up_pre).astype(jnp.bfloat16)
    d_hidden = lax.dot_general(
        slot_grad, down_proj, (((1,), (1,)), ((), ())), preferred_element_type=jnp.float32
    )
    d_gate = d_hidden * up_pre * sigmoid_gate * (1.0 + gate_pre * (1.0 - sigmoid_gate))
    d_up = d_hidden * gate_act
    d_pre = jnp.concatenate([d_gate, d_up], axis=1).astype(jnp.bfloat16)
    slot_back = lax.dot_general(
        d_pre, gate_up, (((1,), (1,)), ((), ())), preferred_element_type=jnp.float32
    ).astype(jnp.bfloat16)
    returned = swap_tokens(slot_back)
    in_grad = lax.dot_general(
        select, returned, (((0,), (0,)), ((), ())), preferred_element_type=jnp.float32
    ).astype(jnp.bfloat16)

    grad_down = lax.dot_general(
        hidden, slot_grad, (((0,), (0,)), ((), ())), preferred_element_type=jnp.float32
    )
    grad_gate_up = lax.dot_general(
        slot_input, d_pre, (((0,), (0,)), ((), ())), preferred_element_type=jnp.float32
    )
    half = model_width // replicas
    mine = replica * half
    other = (1 - replica) * half
    trade = [(0, 1), (1, 0)]
    sent_gate_up = lax.dynamic_slice_in_dim(grad_gate_up, other, half, 0).astype(jnp.bfloat16)
    sent_down = lax.dynamic_slice_in_dim(grad_down, other, half, 1).astype(jnp.bfloat16)
    part_gate_up = lax.dynamic_slice_in_dim(grad_gate_up, mine, half, 0) + lax.ppermute(
        sent_gate_up, "dp", trade
    ).astype(jnp.float32)
    part_down = lax.dynamic_slice_in_dim(grad_down, mine, half, 1) + lax.ppermute(
        sent_down, "dp", trade
    ).astype(jnp.float32)
    local_peak = jnp.maximum(jnp.max(jnp.abs(part_gate_up)), jnp.max(jnp.abs(part_down)))
    peak_abs = lax.pmax(local_peak, "dp")
    scale_by = 1.0 / (peak_abs + PEAK_EPS)
    own_gate_up = lax.dynamic_slice_in_dim(gate_up, mine, half, 0)
    own_down = lax.dynamic_slice_in_dim(down_proj, mine, half, 1)
    updated = adam_update(own_gate_up, part_gate_up, m_gate_up[0], v_gate_up[0], scale_by)
    updated += adam_update(own_down, part_down, m_down[0], v_down[0], scale_by)

    tiles = [to_tiles(u) for u in updated]
    counts = [t.shape[0] for t in tiles]
    total = sum(counts)
    per_piece = -(-total // expert_count)
    spare = per_piece * expert_count - total
    packed = jnp.concatenate(tiles + [jnp.zeros((spare, SUB, LANE), jnp.bfloat16)], axis=0)
    packed = packed.reshape(expert_count, per_piece, SUB, LANE)
    spread = lax.all_to_all(packed, "expert", split_axis=0, concat_axis=0, tiled=True)
    picked = jnp.take(spread, partner, axis=0)
    arrived = lax.all_to_all(picked, "expert", split_axis=0, concat_axis=0, tiled=True)
    arrived = arrived.reshape(-1, SUB, LANE)
    moved = []
    start = 0
    for u, count in zip(updated, counts):
        moved.append(from_tiles(arrived[start : start + count], *u.shape))
        start += count
    new_gu, gate_mean, gate_square, new_dn, down_mean, down_square = moved
    return (
        in_grad,
        new_gu[None],
        new_dn[None],
        gate_mean.astype(jnp.float32)[None],
        gate_square.astype(jnp.float32)[None],
        down_mean.astype(jnp.float32)[None],
        down_square.astype(jnp.float32)[None],
    )


def solution(mesh):
    in_specs = (
        P(("dp", "expert"), None),
        P(("dp", "expert"), None),
        P(("dp", "expert"), None),
        P(("dp", "expert"), None),
        P("expert", None, None),
        P("expert", None, None),
        P("expert", "dp", None),
        P("expert", "dp", None),
        P("expert", None, "dp"),
        P("expert", None, "dp"),
        P(),
    )
    out_specs = (
        P(("dp", "expert"), None),
        P("expert", "dp", None),
        P("expert", None, "dp"),
        P("expert", "dp", None),
        P("expert", "dp", None),
        P("expert", None, "dp"),
        P("expert", None, "dp"),
    )
    return jax.shard_map(
        per_device, mesh=mesh, in_specs=in_specs, out_specs=out_specs, check_vma=False
    )
```

time: 679 us -> 419 us (0.62); the launches traced: 669 us -> 418 us
  starting transfers between devices: 133 us -> 48.2 us
  local copies, waits for them, and re-layouts: 91.6 us -> 17.9 us
  waiting for transfers between devices: 347 us -> 306 us
  other arithmetic: 56.2 us -> 17.7 us
  between operations: 17 us -> 3.01 us
    all_to_all x15 -> x5, starting transfers between devices: 133 us -> 47.7 us  [the longest x3 32.2 us: swap_tokens(): lax.all_to_all(rows.reshape(expert_count, capacity, model_width), 'expert...]
    all_to_all x15 -> x5, waiting for transfers between devices: 330 us -> 304 us  [the longest x3 140 us: swap_tokens(): lax.all_to_all(rows.reshape(expert_count, capacity, model_width), 'expert...]
    unnamed x50 -> x46, local copies, waits for them, and re-layouts: 30.7 us -> 6.14 us
    all_to_all x6 -> x0, other arithmetic: 23.4 us -> none  [the longest x1 5.15 us: move_moments(): lax.all_to_all(picked[0], 'expert', split_axis=0, concat_axis=1, tiled=True)]
    gather x10 -> x1, local copies, waits for them, and re-layouts: 25 us -> 4.91 us  [per_device(): picked = jnp.take(spread, partner, axis=0)]
    reduce_scatter x2 -> x0, waiting for transfers between devices: 16.3 us -> none  [the longest x1 16.2 us: per_device(): lax.psum_scatter(grad_gate_up.astype(jnp.bfloat16), 'dp', scatter_dimensi...]
    reshape x7 -> x0, local copies, waits for them, and re-layouts: 15 us -> none  [the longest x1 4.5 us: move_weights_after(): gate_up.reshape(1, expert_count, -1)]
    select_n x4 -> x1, local copies, waits for them, and re-layouts: 10.2 us -> 0.09 us  [slot_select(): place = jnp.where(member, rank.astype(jnp.int32), -1)]
  transfers between devices with their start and end apart: 17 -> 7, of which waited for: 15 -> 6; matrix products, arithmetic and copies ran while one was open for 19% -> 6% of each run, Pallas kernels for 0% -> 0%
where the time goes in v1:
time: 419 us; the launch traced here: 418 us
  waiting for transfers between devices  306 us (73%)
  starting transfers between devices  48.2 us (12%)
  matrix products  22.3 us (5%)
  local copies, waits for them, and re-layouts  17.9 us (4%)
  other arithmetic  17.7 us (4%)
    all_to_all x3, waiting for transfers between devices, swap_tokens(): lax.all_to_all(rows.reshape(expert_count, capacity, model_width), 'expert...  140 us
    all_to_all x1, waiting for transfers between devices, per_device(): lax.all_to_all(picked, 'expert', split_axis=0, concat_axis=0, tiled=True)  83.3 us
    all_to_all x1, waiting for transfers between devices, per_device(): lax.all_to_all(packed, 'expert', split_axis=0, concat_axis=0, tiled=True)  81.4 us
    all_to_all x3, starting transfers between devices, swap_tokens(): lax.all_to_all(rows.reshape(expert_count, capacity, model_width), 'expert...  32.2 us
  transfers between devices with their start and end apart: 7, of which 6 were waited for; matrix products, arithmetic and copies ran while one was open for 6% of the time, Pallas kernels for 0%

profile of v1, /device:TPU:2, one launch (start us, length us, event | category | flops | bytes accessed | tf_op | source)
XLA Modules:
  0.0 418.1 jit_solution(13464679283168917306)
XLA Ops:
  0.7 0.8 copy.31
  1.5 0.2 fusion.30
  1.6 0.2 fusion.17
  2.0 2.1 convert_bitcast_fusion.1
  4.1 15.6 %all-to-all-start.1 = ((bf16[128,8,1024]{2,1,0:T(8,128)(2,1)}), bf16[128,8,1024]{2,1,0:T(8,128)(2,1)S(1)}, u32[]{:S(2)}, u32[]{:S(2)}) async-start(bf16[128,8,1024]{2,1,0:T(8,128)(2,1)} %convert_bitcast_fusion.1), calls=%async_computation.1 | async-start | bytes 4194304 | tf_op jit(solution)/shard_map/all_to_all | solution.py:97
  19.8 0.2 select_reduce_fusion.1
  20.1 0.2 select_reduce_fusion
  20.4 2.1 fusion.8
  22.6 49.8 %all-to-all-done.1 = bf16[128,8,1024]{2,1,0:T(8,128)(2,1)S(1)} async-done(((bf16[128,8,1024]{2,1,0:T(8,128)(2,1)}), bf16[128,8,1024]{2,1,0:T(8,128)(2,1)S(1)}, u32[]{:S(2)}, u32[]{:S(2)}) %all-to-all-start.1) | async-done | bytes 2097184 | tf_op jit(solution)/shard_map/all_to_all | solution.py:97
  72.3 7.7 %all-to-all-start = ((bf16[128,8,1024]{2,1,0:T(8,128)(2,1)}), bf16[128,8,1024]{2,1,0:T(8,128)(2,1)}, u32[]{:S(2)}, u32[]{:S(2)}) async-start(bf16[128,8,1024]{2,1,0:T(8,128)(2,1)} %fusion.8), calls=%async_computation | async-start | bytes 4194304 | tf_op jit(solution)/shard_map/all_to_all | solution.py:97
  80.1 5.0 %fusion.2 = f32[1024,768]{0,1:T(8,128)} fusion(bf16[128,8,1024]{2,1,0:T(8,128)(2,1)S(1)} %all-to-all-done.1, bf16[1,1024,768]{2,1,0:T(8,128)(2,1)} %param.15), kind=kOutput, calls=%fused_computation.6 | convolution fusion | flops 1610612736 | bytes 6815744 | tf_op jit(solution)/shard_map/dot_general | solution.py:115
  85.0 46.5 %all-to-all-done = bf16[128,8,1024]{2,1,0:T(8,128)(2,1)} async-done(((bf16[128,8,1024]{2,1,0:T(8,128)(2,1)}), bf16[128,8,1024]{2,1,0:T(8,128)(2,1)}, u32[]{:S(2)}, u32[]{:S(2)}) %all-to-all-start) | async-done | bytes 2097184 | tf_op jit(solution)/shard_map/all_to_all | solution.py:97
  131.6 4.1 multiply_convert_fusion.3
  135.7 1.9 fusion
  137.6 1.0 dynamic-slice_convert_fusion
  138.5 2.6 fusion.4
  141.2 1.1 copy-done.2
  142.3 0.8 dynamic-slice_convert_fusion.1
  143.1 0.5 collective-permute-start.1
  143.6 1.7 collective-permute-done.1
  145.3 2.0 abs_reduce_fusion.1
  147.3 1.9 abs_reduce_fusion
  150.5 3.0 pmax.7
  154.2 3.8 fusion.24
  158.1 0.1 constant_dynamic-update-slice_fusion.4
  158.2 0.1 constant_dynamic-update-slice_fusion.3
  158.3 0.8 copy-done.10
  159.1 0.5 copy-done.3
  159.7 0.2 copy-done.6
  159.9 0.2 copy-done.7
  160.1 1.7 fusion.33
  162.0 1.8 copy-done.1
  163.9 7.8 %all-to-all-start.3 = ((bf16[128,14,8,128]{3,2,1,0:T(8,128)(2,1)}), bf16[128,14,8,128]{3,2,1,0:T(8,128)(2,1)}, u32[]{:S(2)}, u32[]{:S(2)}) async-start(bf16[128,14,8,128]{3,2,1,0:T(8,128)(2,1)} %bitcast.155), calls=%async_computation.3 | async-start | bytes 7340032 | tf_op jit(solution)/shard_map/all_to_all | solution.py:168
  171.8 3.2 convert_bitcast_fusion
  175.0 81.4 %all-to-all-done.3 = bf16[128,14,8,128]{3,2,1,0:T(8,128)(2,1)} async-done(((bf16[128,14,8,128]{3,2,1,0:T(8,128)(2,1)}), bf16[128,14,8,128]{3,2,1,0:T(8,128)(2,1)}, u32[]{:S(2)}, u32[]{:S(2)}) %all-to-all-start.3) | async-done | bytes 3670048 | tf_op jit(solution)/shard_map/all_to_all | solution.py:168
  256.4 8.9 %all-to-all-start.2 = ((bf16[128,8,1024]{2,1,0:T(8,128)(2,1)}), bf16[128,8,1024]{2,1,0:T(8,128)(2,1)S(1)}, u32[]{:S(2)}, u32[]{:S(2)}) async-start(bf16[128,8,1024]{2,1,0:T(8,128)(2,1)} %convert_bitcast_fusion), calls=%async_computation.2 | async-start | bytes 4194304 | tf_op jit(solution)/shard_map/all_to_all | solution.py:97
  265.4 0.1 add_reduce_fusion
  265.4 0.1 fusion.38
  265.6 4.9 %gather_fusion = bf16[128,14,8,128]{3,2,1,0:T(8,128)(2,1)} fusion(bf16[128,14,8,128]{3,2,1,0:T(8,128)(2,1)} %all-to-all-done.3, s32[1024]{0:T(1024)S(1)} %pad_clamp_fusion), kind=kCustom, calls=%fused_computation | custom fusion | bytes 7340544 | tf_op jit(solution)/shard_map/jit(_take)/gather | solution.py:169
  270.5 4.3 %broadcast_select_fusion = bf16[128,14,8,128]{3,2,1,0:T(8,128)(2,1)} fusion(bf16[128,14,8,128]{3,2,1,0:T(8,128)(2,1)} %gather_fusion, pred[128]{0:T(512)(128)(4,1)S(1)} %compare_and_fusion), kind=kLoop, calls=%fused_computation.2 | loop fusion | flops 1835008 | bytes 7340160 | tf_op jit(solution)/shard_map/jit(_take)/select_n | solution.py:169
  274.8 43.2 %all-to-all-done.2 = bf16[128,8,1024]{2,1,0:T(8,128)(2,1)S(1)} async-done(((bf16[128,8,1024]{2,1,0:T(8,128)(2,1)}), bf16[128,8,1024]{2,1,0:T(8,128)(2,1)S(1)}, u32[]{:S(2)}, u32[]{:S(2)}) %all-to-all-start.2) | async-done | bytes 2097184 | tf_op jit(solution)/shard_map/all_to_all | solution.py:97
  318.0 7.7 %all-to-all-start.4 = ((bf16[128,14,8,128]{3,2,1,0:T(8,128)(2,1)}), bf16[128,14,8,128]{3,2,1,0:T(8,128)(2,1)}, u32[]{:S(2)}, u32[]{:S(2)}) async-start(bf16[128,14,8,128]{3,2,1,0:T(8,128)(2,1)} %broadcast_select_fusion), calls=%async_computation.4 | async-start | bytes 7340032 | tf_op jit(solution)/shard_map/all_to_all | solution.py:170
  325.6 1.2 fusion.16
  326.8 83.3 %all-to-all-done.4 = bf16[128,14,8,128]{3,2,1,0:T(8,128)(2,1)} async-done(((bf16[128,14,8,128]{3,2,1,0:T(8,128)(2,1)}), bf16[128,14,8,128]{3,2,1,0:T(8,128)(2,1)}, u32[]{:S(2)}, u32[]{:S(2)}) %all-to-all-start.4) | async-done | bytes 3670048 | tf_op jit(solution)/shard_map/all_to_all | solution.py:170
  410.1 2.1 fusion.47
  412.2 2.6 fusion.48
  414.8 1.4 convert_bitcast_fusion.4
  416.2 1.9 convert_bitcast_fusion.2
  (50 shorter events, 0.8 us)
Async XLA Ops:
  0.6 1.4 copy-start
  4.1 15.6 %copy-start.12 = (f32[64,8]{0,1:T(8,128)S(1)}, f32[64,8]{0,1:T(8,128)}, u32[]{:S(2)}) copy-start(f32[64,8]{0,1:T(8,128)} %param.13) | copy-start | bytes 6148
  4.1 16.3 %copy-start.11 = (bf16[64,1024]{1,0:T(8,128)(2,1)S(1)}, bf16[64,1024]{1,0:T(8,128)(2,1)}, u32[]{:S(2)}) copy-start(bf16[64,1024]{1,0:T(8,128)(2,1)} %param.11) | copy-start | bytes 393220
  4.1 68.2 %all-to-all-start.1 = ((bf16[128,8,1024]{2,1,0:T(8,128)(2,1)}), bf16[128,8,1024]{2,1,0:T(8,128)(2,1)S(1)}, u32[]{:S(2)}, u32[]{:S(2)}) async-start(bf16[128,8,1024]{2,1,0:T(8,128)(2,1)} %convert_bitcast_fusion.1), calls=%async_computation.1 | async-start | bytes 4194304 | tf_op jit(solution)/shard_map/all_to_all | solution.py:97
  72.3 7.7 %copy-start.4 = (bf16[128,8,1024]{2,1,0:T(8,128)(2,1)}, bf16[128,8,1024]{2,1,0:T(8,128)(2,1)S(1)}, u32[]{:S(2)}) copy-start(bf16[128,8,1024]{2,1,0:T(8,128)(2,1)S(1)} %all-to-all-done.1) | copy-start | bytes 6291460
  72.3 59.2 %all-to-all-start = ((bf16[128,8,1024]{2,1,0:T(8,128)(2,1)}), bf16[128,8,1024]{2,1,0:T(8,128)(2,1)}, u32[]{:S(2)}, u32[]{:S(2)}) async-start(bf16[128,8,1024]{2,1,0:T(8,128)(2,1)} %fusion.8), calls=%async_computation | async-start | bytes 4194304 | tf_op jit(solution)/shard_map/all_to_all | solution.py:97
  80.1 51.5 %copy-start.9 = (bf16[1,384,1024]{2,1,0:T(8,128)(2,1)S(1)}, bf16[1,384,1024]{2,1,0:T(8,128)(2,1)}, u32[]{:S(2)}) copy-start(bf16[1,384,1024]{2,1,0:T(8,128)(2,1)} %param.16) | copy-start | bytes 2359300
  131.6 4.1 copy-start.5
  135.6 1.9 copy-start.15
  135.7 1.9 copy-start.17
  135.7 2.9 copy-start.14
  138.5 8.8 %collective-permute-start = (bf16[512,768]{1,0:T(8,128)(2,1)}, bf16[512,768]{1,0:T(8,128)(2,1)}, u32[]{:S(2)}, u32[]{:S(2)}) collective-permute-start(bf16[512,768]{1,0:T(8,128)(2,1)} %dynamic-slice_convert_fusion), channel_id=1, source_target_pairs={{0,128},{128,0},{1,129},{129,1},{2,130},{130,2},{3,131},{131,3},{4... | collective-permute-start | bytes 2359304 | tf_op jit(solution)/shard_map/ppermute | solution.py:147
  141.2 1.1 copy-start.2
  143.1 2.2 collective-permute-start.1
  158.0 1.1 copy-start.10
  158.1 1.6 copy-start.3
  158.1 1.8 copy-start.6
  158.1 2.0 copy-start.7
  162.0 1.8 copy-start.1
  163.9 7.9 %copy-start.8 = (bf16[1,1024,768]{2,1,0:T(8,128)(2,1)S(1)}, bf16[1,1024,768]{2,1,0:T(8,128)(2,1)}, u32[]{:S(2)}) copy-start(bf16[1,1024,768]{2,1,0:T(8,128)(2,1)} %param.15) | copy-start | bytes 4718596
  163.9 7.9 %copy-start.16 = (bf16[1024,384]{0,1:T(8,128)(2,1)S(1)}, bf16[1024,384]{0,1:T(8,128)(2,1)}, u32[]{:S(2)}) copy-start(bf16[1024,384]{0,1:T(8,128)(2,1)} %copy-done.15) | copy-start | bytes 2359300
  163.9 7.9 %copy-start.18 = (bf16[1024,384]{0,1:T(8,128)(2,1)S(1)}, bf16[1024,384]{0,1:T(8,128)(2,1)}, u32[]{:S(2)}) copy-start(bf16[1024,384]{0,1:T(8,128)(2,1)} %copy-done.17) | copy-start | bytes 2359300
  163.9 92.6 %all-to-all-start.3 = ((bf16[128,14,8,128]{3,2,1,0:T(8,128)(2,1)}), bf16[128,14,8,128]{3,2,1,0:T(8,128)(2,1)}, u32[]{:S(2)}, u32[]{:S(2)}) async-start(bf16[128,14,8,128]{3,2,1,0:T(8,128)(2,1)} %bitcast.155), calls=%async_computation.3 | async-start | bytes 7340032 | tf_op jit(solution)/shard_map/all_to_all | solution.py:168
  175.0 90.3 %copy-start.13 = (s32[32,2]{0,1:T(2,128)S(1)}, s32[32,2]{0,1:T(2,128)}, u32[]{:S(2)}) copy-start(s32[32,2]{0,1:T(2,128)} %param.21) | copy-start | bytes 772
  256.4 61.6 %all-to-all-start.2 = ((bf16[128,8,1024]{2,1,0:T(8,128)(2,1)}), bf16[128,8,1024]{2,1,0:T(8,128)(2,1)S(1)}, u32[]{:S(2)}, u32[]{:S(2)}) async-start(bf16[128,8,1024]{2,1,0:T(8,128)(2,1)} %convert_bitcast_fusion), calls=%async_computation.2 | async-start | bytes 4194304 | tf_op jit(solution)/shard_map/all_to_all | solution.py:97
  318.0 92.1 %all-to-all-start.4 = ((bf16[128,14,8,128]{3,2,1,0:T(8,128)(2,1)}), bf16[128,14,8,128]{3,2,1,0:T(8,128)(2,1)}, u32[]{:S(2)}, u32[]{:S(2)}) async-start(bf16[128,14,8,128]{3,2,1,0:T(8,128)(2,1)} %broadcast_select_fusion), calls=%async_computation.4 | async-start | bytes 7340032 | tf_op jit(solution)/shard_map/all_to_all | solution.py:170

commit v2 on v1

--- a/solution.py
+++ b/solution.py
@@ -127,10 +127,8 @@
     slot_back = lax.dot_general(
         d_pre, gate_up, (((1,), (1,)), ((), ())), preferred_element_type=jnp.float32
     ).astype(jnp.bfloat16)
+    slot_back, d_pre, hidden = lax.optimization_barrier((slot_back, d_pre, hidden))
     returned = swap_tokens(slot_back)
-    in_grad = lax.dot_general(
-        select, returned, (((0,), (0,)), ((), ())), preferred_element_type=jnp.float32
-    ).astype(jnp.bfloat16)
 
     grad_down = lax.dot_general(
         hidden, slot_grad, (((0,), (0,)), ((), ())), preferred_element_type=jnp.float32
@@ -165,8 +163,12 @@
     spare = per_piece * expert_count - total
     packed = jnp.concatenate(tiles + [jnp.zeros((spare, SUB, LANE), jnp.bfloat16)], axis=0)
     packed = packed.reshape(expert_count, per_piece, SUB, LANE)
+    packed, returned = lax.optimization_barrier((packed, returned))
     spread = lax.all_to_all(packed, "expert", split_axis=0, concat_axis=0, tiled=True)
-    picked = jnp.take(spread, partner, axis=0)
+    in_grad = lax.dot_general(
+        select, returned, (((0,), (0,)), ((), ())), preferred_element_type=jnp.float32
+    ).astype(jnp.bfloat16)
+    picked = spread.at[partner].get(mode="promise_in_bounds")
     arrived = lax.all_to_all(picked, "expert", split_axis=0, concat_axis=0, tiled=True)
     arrived = arrived.reshape(-1, SUB, LANE)
     moved = []

time: 419 us -> 396 us (0.945)
  waiting for transfers between devices: 306 us -> 283 us
    all_to_all x3, waiting for transfers between devices: 140 us -> 116 us  [swap_tokens(): lax.all_to_all(rows.reshape(expert_count, capacity, model_width), 'expert...]
    select_n x2 -> x1, other arithmetic: 4.29 us -> 0.01 us  [per_device(): picked = spread.at[partner].get(mode='promise_in_bounds')]
    unnamed x46 -> x36, local copies, waits for them, and re-layouts: 6.14 us -> 8.49 us
  transfers between devices with their start and end apart: 7 -> 7, of which waited for: 6 -> 6; matrix products, arithmetic and copies ran while one was open for 6% -> 8% of each run, Pallas kernels for 0% -> 0%
where the time goes in v2:
time: 396 us
  waiting for transfers between devices  283 us (71%)
  starting transfers between devices  46.8 us (12%)
  matrix products  25.3 us (6%)
  local copies, waits for them, and re-layouts  21 us (5%)
  other arithmetic  14 us (4%)
    all_to_all x3, waiting for transfers between devices, swap_tokens(): lax.all_to_all(rows.reshape(expert_count, capacity, model_width), 'expert...  116 us
    all_to_all x1, waiting for transfers between devices, per_device(): lax.all_to_all(packed, 'expert', split_axis=0, concat_axis=0, tiled=True)  83 us
    all_to_all x1, waiting for transfers between devices, per_device(): lax.all_to_all(picked, 'expert', split_axis=0, concat_axis=0, tiled=True)  81.4 us
    all_to_all x3, starting transfers between devices, swap_tokens(): lax.all_to_all(rows.reshape(expert_count, capacity, model_width), 'expert...  30.6 us
    all_to_all x1, starting transfers between devices, per_device(): lax.all_to_all(picked, 'expert', split_axis=0, concat_axis=0, tiled=True)  8.56 us
    unnamed x36, local copies, waits for them, and re-layouts  8.49 us
  transfers between devices with their start and end apart: 7, of which 6 were waited for; matrix products, arithmetic and copies ran while one was open for 8% of the time, Pallas kernels for 0%

profile of v2, /device:TPU:2, one launch (start us, length us, event | category | flops | bytes accessed | tf_op | source)
XLA Modules:
  0.0 395.5 jit_solution(12460551234050780289)
XLA Ops:
  0.7 0.8 copy.27
  1.5 0.2 fusion.30
  1.6 0.2 fusion.16
  2.0 2.1 convert_bitcast_fusion
  4.1 15.6 %all-to-all-start = ((bf16[128,8,1024]{2,1,0:T(8,128)(2,1)}), bf16[128,8,1024]{2,1,0:T(8,128)(2,1)S(1)}, u32[]{:S(2)}, u32[]{:S(2)}) async-start(bf16[128,8,1024]{2,1,0:T(8,128)(2,1)} %convert_bitcast_fusion), calls=%async_computation | async-start | bytes 4194304 | tf_op jit(solution)/shard_map/all_to_all | solution.py:97
  19.8 0.2 select_reduce_fusion.1
  20.1 0.2 select_reduce_fusion
  20.4 2.2 fusion.8
  22.6 49.7 %all-to-all-done = bf16[128,8,1024]{2,1,0:T(8,128)(2,1)S(1)} async-done(((bf16[128,8,1024]{2,1,0:T(8,128)(2,1)}), bf16[128,8,1024]{2,1,0:T(8,128)(2,1)S(1)}, u32[]{:S(2)}, u32[]{:S(2)}) %all-to-all-start) | async-done | bytes 2097184 | tf_op jit(solution)/shard_map/all_to_all | solution.py:97
  72.3 7.7 %all-to-all-start.1 = ((bf16[128,8,1024]{2,1,0:T(8,128)(2,1)}), bf16[128,8,1024]{2,1,0:T(8,128)(2,1)}, u32[]{:S(2)}, u32[]{:S(2)}) async-start(bf16[128,8,1024]{2,1,0:T(8,128)(2,1)} %fusion.8), calls=%async_computation.1 | async-start | bytes 4194304 | tf_op jit(solution)/shard_map/all_to_all | solution.py:97
  80.1 5.0 %fusion.6 = f32[1024,768]{0,1:T(8,128)} fusion(bf16[128,8,1024]{2,1,0:T(8,128)(2,1)S(1)} %all-to-all-done, bf16[1,1024,768]{2,1,0:T(8,128)(2,1)} %param.15), kind=kOutput, calls=%fused_computation.9 | convolution fusion | flops 1610612736 | bytes 6815744 | tf_op jit(solution)/shard_map/dot_general | solution.py:115
  85.0 46.5 %all-to-all-done.1 = bf16[128,8,1024]{2,1,0:T(8,128)(2,1)} async-done(((bf16[128,8,1024]{2,1,0:T(8,128)(2,1)}), bf16[128,8,1024]{2,1,0:T(8,128)(2,1)}, u32[]{:S(2)}, u32[]{:S(2)}) %all-to-all-start.1) | async-done | bytes 2097184 | tf_op jit(solution)/shard_map/all_to_all | solution.py:97
  131.6 4.9 %multiply_convert_fusion.3 = (bf16[1024,384]{0,1:T(8,128)(2,1)S(1)}, bf16[1024,384]{0,1:T(8,128)(2,1)S(1)}, bf16[1024,384]{0,1:T(8,128)(2,1)}) fusion(f32[1024,768]{0,1:T(8,128)} %fusion.6, bf16[1,384,1024]{2,1,0:T(8,128)(2,1)S(1)} %copy-done.8, bf16[128,8,1024]{2,1,0:T(8,128)(2,1)} %all-to-all-done.1), kind=kOutput, calls=%fused_computation.31 | convolution fusion | flops 811204608 | bytes 8388608 | tf_op jit(solution)/shard_map/dot_general | solution.py:121
  136.5 1.3 pad_maximum_fusion
  137.7 0.7 copy-done.7
  138.5 3.3 convolution_convert_fusion
  141.7 7.4 %all-to-all-start.2 = ((bf16[128,8,1024]{2,1,0:T(8,128)(2,1)}), bf16[128,8,1024]{2,1,0:T(8,128)(2,1)S(1)}, u32[]{:S(2)}, u32[]{:S(2)}) async-start(bf16[128,8,1024]{2,1,0:T(8,128)(2,1)} %bitcast.160), calls=%async_computation.2 | async-start | bytes 4194304 | tf_op jit(solution)/shard_map/all_to_all | solution.py:97
  149.1 3.9 fusion.4
  153.0 1.0 dynamic-slice_convert_fusion
  154.0 0.7 copy-done.13
  154.7 2.6 fusion
  157.3 0.9 dynamic-slice_convert_fusion.1
  158.2 0.4 copy-done.2
  158.6 1.9 collective-permute-done.1
  160.5 1.8 abs_reduce_fusion.1
  162.3 2.1 abs_reduce_fusion
  165.8 3.0 pmax.7
  169.4 3.9 fusion.23
  173.4 0.9 constant_dynamic-update-slice_fusion.5
  174.3 0.9 constant_dynamic-update-slice_fusion.4
  175.2 1.0 constant_dynamic-update-slice_fusion.3
  176.2 0.5 copy-done.6
  176.8 0.7 fusion.32
  177.5 0.8 constant_dynamic-update-slice_fusion.2
  178.3 0.8 constant_dynamic-update-slice_fusion.1
  179.1 0.8 constant_dynamic-update-slice_fusion
  179.9 0.7 broadcast_dynamic-update-slice_fusion
  180.5 20.0 %all-to-all-done.2 = bf16[128,8,1024]{2,1,0:T(8,128)(2,1)S(1)} async-done(((bf16[128,8,1024]{2,1,0:T(8,128)(2,1)}), bf16[128,8,1024]{2,1,0:T(8,128)(2,1)S(1)}, u32[]{:S(2)}, u32[]{:S(2)}) %all-to-all-start.2) | async-done | bytes 2097184 | tf_op jit(solution)/shard_map/all_to_all | solution.py:97
  200.5 7.6 %all-to-all-start.3 = ((bf16[128,14,8,128]{3,2,1,0:T(8,128)(2,1)}), bf16[128,14,8,128]{3,2,1,0:T(8,128)(2,1)}, u32[]{:S(2)}, u32[]{:S(2)}) async-start(bf16[128,14,8,128]{3,2,1,0:T(8,128)(2,1)} %bitcast.35), calls=%async_computation.3 | async-start | bytes 7340032 | tf_op jit(solution)/shard_map/all_to_all | solution.py:167
  208.4 83.0 %all-to-all-done.3 = bf16[128,14,8,128]{3,2,1,0:T(8,128)(2,1)} async-done(((bf16[128,14,8,128]{3,2,1,0:T(8,128)(2,1)}), bf16[128,14,8,128]{3,2,1,0:T(8,128)(2,1)}, u32[]{:S(2)}, u32[]{:S(2)}) %all-to-all-start.3) | async-done | bytes 3670048 | tf_op jit(solution)/shard_map/all_to_all | solution.py:167
  291.4 4.9 %gather_fusion = bf16[128,14,8,128]{3,2,1,0:T(8,128)(2,1)} fusion(bf16[128,14,8,128]{3,2,1,0:T(8,128)(2,1)} %all-to-all-done.3, s32[1024]{0:T(1024)S(1)} %pad_clamp_fusion), kind=kCustom, calls=%fused_computation | custom fusion | bytes 7340544 | tf_op jit(solution)/shard_map/gather | solution.py:171
  296.3 8.6 %all-to-all-start.4 = ((bf16[128,14,8,128]{3,2,1,0:T(8,128)(2,1)}), bf16[128,14,8,128]{3,2,1,0:T(8,128)(2,1)}, u32[]{:S(2)}, u32[]{:S(2)}) async-start(bf16[128,14,8,128]{3,2,1,0:T(8,128)(2,1)} %gather_fusion), calls=%async_computation.4 | async-start | bytes 7340032 | tf_op jit(solution)/shard_map/all_to_all | solution.py:172
  304.9 1.3 convolution_convert_fusion.1
  306.2 81.4 %all-to-all-done.4 = bf16[128,14,8,128]{3,2,1,0:T(8,128)(2,1)} async-done(((bf16[128,14,8,128]{3,2,1,0:T(8,128)(2,1)}), bf16[128,14,8,128]{3,2,1,0:T(8,128)(2,1)}, u32[]{:S(2)}, u32[]{:S(2)}) %all-to-all-start.4) | async-done | bytes 3670048 | tf_op jit(solution)/shard_map/all_to_all | solution.py:172
  387.6 2.1 fusion.43
  389.6 2.6 fusion.44
  392.3 1.4 convert_bitcast_fusion.3
  393.6 1.9 convert_bitcast_fusion.1
  (39 shorter events, 0.8 us)
Async XLA Ops:
  0.6 1.4 copy-start
  4.1 15.6 %copy-start.11 = (f32[64,8]{0,1:T(8,128)S(1)}, f32[64,8]{0,1:T(8,128)}, u32[]{:S(2)}) copy-start(f32[64,8]{0,1:T(8,128)} %param.13) | copy-start | bytes 6148
  4.1 16.3 %copy-start.10 = (bf16[64,1024]{1,0:T(8,128)(2,1)S(1)}, bf16[64,1024]{1,0:T(8,128)(2,1)}, u32[]{:S(2)}) copy-start(bf16[64,1024]{1,0:T(8,128)(2,1)} %param.11) | copy-start | bytes 393220
  4.1 68.2 %all-to-all-start = ((bf16[128,8,1024]{2,1,0:T(8,128)(2,1)}), bf16[128,8,1024]{2,1,0:T(8,128)(2,1)S(1)}, u32[]{:S(2)}, u32[]{:S(2)}) async-start(bf16[128,8,1024]{2,1,0:T(8,128)(2,1)} %convert_bitcast_fusion), calls=%async_computation | async-start | bytes 4194304 | tf_op jit(solution)/shard_map/all_to_all | solution.py:97
  72.3 7.7 %copy-start.4 = (bf16[128,8,1024]{2,1,0:T(8,128)(2,1)}, bf16[128,8,1024]{2,1,0:T(8,128)(2,1)S(1)}, u32[]{:S(2)}) copy-start(bf16[128,8,1024]{2,1,0:T(8,128)(2,1)S(1)} %all-to-all-done) | copy-start | bytes 6291460
  72.3 59.2 %all-to-all-start.1 = ((bf16[128,8,1024]{2,1,0:T(8,128)(2,1)}), bf16[128,8,1024]{2,1,0:T(8,128)(2,1)}, u32[]{:S(2)}, u32[]{:S(2)}) async-start(bf16[128,8,1024]{2,1,0:T(8,128)(2,1)} %fusion.8), calls=%async_computation.1 | async-start | bytes 4194304 | tf_op jit(solution)/shard_map/all_to_all | solution.py:97
  80.1 51.5 %copy-start.8 = (bf16[1,384,1024]{2,1,0:T(8,128)(2,1)S(1)}, bf16[1,384,1024]{2,1,0:T(8,128)(2,1)}, u32[]{:S(2)}) copy-start(bf16[1,384,1024]{2,1,0:T(8,128)(2,1)} %param.16) | copy-start | bytes 2359300
  136.5 2.0 copy-start.7
  141.7 58.8 %all-to-all-start.2 = ((bf16[128,8,1024]{2,1,0:T(8,128)(2,1)}), bf16[128,8,1024]{2,1,0:T(8,128)(2,1)S(1)}, u32[]{:S(2)}, u32[]{:S(2)}) async-start(bf16[128,8,1024]{2,1,0:T(8,128)(2,1)} %bitcast.160), calls=%async_computation.2 | async-start | bytes 4194304 | tf_op jit(solution)/shard_map/all_to_all | solution.py:97
  153.0 4.3 %copy-start.1 = (f32[1024,768]{1,0:T(8,128)}, f32[1024,768]{1,0:T(8,128)S(1)}, u32[]{:S(2)}) copy-start(f32[1024,768]{1,0:T(8,128)S(1)} %fusion.4) | copy-start | bytes 9437188
  153.0 1.7 copy-start.13
  154.0 8.3 %collective-permute-start = (bf16[512,768]{1,0:T(8,128)(2,1)}, bf16[512,768]{1,0:T(8,128)(2,1)S(1)}, u32[]{:S(2)}, u32[]{:S(2)}) collective-permute-start(bf16[512,768]{1,0:T(8,128)(2,1)} %dynamic-slice_convert_fusion), channel_id=1, source_target_pairs={{0,128},{128,0},{1,129},{129,1},{2,130},{130,2},{3,131},{131,3},{4... | collective-permute-start | bytes 2359304 | tf_op jit(solution)/shard_map/ppermute | solution.py:145
  157.3 1.3 copy-start.2
  158.6 1.9 collective-permute-start.1
  173.4 2.8 copy-start.9
  174.3 1.9 copy-start.3
  174.3 1.9 copy-start.5
  174.3 2.5 copy-start.6
  200.5 7.6 %copy-start.12 = (s32[32,2]{0,1:T(2,128)S(1)}, s32[32,2]{0,1:T(2,128)}, u32[]{:S(2)}) copy-start(s32[32,2]{0,1:T(2,128)} %param.21) | copy-start | bytes 772
  200.5 90.9 %all-to-all-start.3 = ((bf16[128,14,8,128]{3,2,1,0:T(8,128)(2,1)}), bf16[128,14,8,128]{3,2,1,0:T(8,128)(2,1)}, u32[]{:S(2)}, u32[]{:S(2)}) async-start(bf16[128,14,8,128]{3,2,1,0:T(8,128)(2,1)} %bitcast.35), calls=%async_computation.3 | async-start | bytes 7340032 | tf_op jit(solution)/shard_map/all_to_all | solution.py:167
  296.3 91.3 %all-to-all-start.4 = ((bf16[128,14,8,128]{3,2,1,0:T(8,128)(2,1)}), bf16[128,14,8,128]{3,2,1,0:T(8,128)(2,1)}, u32[]{:S(2)}, u32[]{:S(2)}) async-start(bf16[128,14,8,128]{3,2,1,0:T(8,128)(2,1)} %gather_fusion), calls=%async_computation.4 | async-start | bytes 7340032 | tf_op jit(solution)/shard_map/all_to_all | solution.py:172

commit v3 on v2

--- a/solution.py
+++ b/solution.py
@@ -1,6 +1,10 @@
+import functools
+
 import jax
 import jax.numpy as jnp
 from jax import lax
+from jax.experimental import pallas as pl
+from jax.experimental.pallas import tpu as pltpu
 from jax.sharding import PartitionSpec as P
 
 BETA_ONE = 0.9
@@ -11,6 +15,7 @@
 PEAK_EPS = 1e-06
 SUB = 8
 LANE = 128
+PLANE = 16
 
 
 def partner_table(swap_pairs, expert_count):
@@ -27,20 +32,114 @@
     return jnp.where(paired, other, devices)
 
 
-def slot_select(routes, combine, expert_count, capacity):
+def home_select(routes, expert_count, capacity):
     tok_rows = routes.shape[0]
     experts = jnp.arange(expert_count, dtype=jnp.int32)
-    hit = routes[:, :, None] == experts[None, None, :]
-    member = jnp.any(hit, axis=1)
-    weight = jnp.sum(jnp.where(hit, combine[:, :, None], jnp.float32(0.0)), axis=1)
+    member = jnp.any(routes[:, :, None] == experts[None, None, :], axis=1)
     earlier = jnp.tril(jnp.ones((tok_rows, tok_rows), jnp.bfloat16), -1)
     rank = jnp.dot(earlier, member.astype(jnp.bfloat16), preferred_element_type=jnp.float32)
     place = jnp.where(member, rank.astype(jnp.int32), -1)
     slots = jnp.arange(capacity, dtype=jnp.int32)
     chosen = place.T[:, None, :] == slots[None, :, None]
-    slot_weight = jnp.sum(jnp.where(chosen, weight.T[:, None, :], jnp.float32(0.0)), axis=2)
-    select = chosen.astype(jnp.bfloat16).reshape(expert_count * capacity, tok_rows)
-    return select, slot_weight.reshape(expert_count * capacity)
+    return chosen.astype(jnp.bfloat16).reshape(expert_count * capacity, tok_rows)
+
+
+def column_select(routes, combine, first_expert, plane, sources, capacity):
+    top_count, columns = routes.shape
+    tok_rows = columns // sources
+    wanted = first_expert + jnp.arange(plane, dtype=jnp.int32)
+    hit = routes[:, None, :] == wanted[None, :, None]
+    member = jnp.any(hit, axis=0)
+    weight = jnp.sum(jnp.where(hit, combine[:, None, :], jnp.float32(0.0)), axis=0)
+    column = jnp.arange(columns, dtype=jnp.int32)
+    source = column // tok_rows
+    earlier = (column[:, None] < column[None, :]) & (source[:, None] == source[None, :])
+    rank = jnp.dot(
+        member.astype(jnp.bfloat16),
+        earlier.astype(jnp.bfloat16),
+        preferred_element_type=jnp.float32,
+    )
+    code = jnp.where(member, source[None, :] * capacity + rank.astype(jnp.int32), -1)
+    slots = jnp.arange(sources * capacity, dtype=jnp.int32)
+    chosen = code[:, None, :] == slots[None, :, None]
+    slot_weight = jnp.sum(jnp.where(chosen, weight[:, None, :], jnp.float32(0.0)), axis=2)
+    select = chosen.astype(jnp.bfloat16).reshape(plane * sources * capacity, columns)
+    return select, slot_weight.reshape(-1)
+
+
+def ring_kernel(depth, plane, *refs):
+    ins = refs[:3]
+    outs = refs[3:6]
+    send_sem, recv_sem = refs[6:]
+    me = lax.axis_index("expert")
+    layer = me // plane
+    spot = me % plane
+    ahead = ((layer + 1) % depth) * plane + spot
+    behind = ((layer + depth - 1) % depth) * plane + spot
+    targets = (ahead, behind)
+
+    barrier = pltpu.get_barrier_semaphore()
+    for target in targets:
+        pl.semaphore_signal(
+            barrier, inc=1, device_id={"expert": target}, device_id_type=pl.DeviceIdType.MESH
+        )
+    pl.semaphore_wait(barrier, 2)
+
+    half = depth // 2
+
+    def copy_of(way, step, which):
+        if way == 0:
+            block = (layer + depth - step) % depth
+        else:
+            block = (layer + step) % depth
+        source = ins[which] if step == 0 else outs[which].at[block]
+        return pltpu.make_async_remote_copy(
+            src_ref=source,
+            dst_ref=outs[which].at[block],
+            send_sem=send_sem.at[way, step, which],
+            recv_sem=recv_sem.at[way, step, which],
+            device_id={"expert": targets[way]},
+            device_id_type=pl.DeviceIdType.MESH,
+        )
+
+    started = []
+    previous = {}
+    for step in range(half):
+        for which in (2, 0, 1):
+            for way in (0, 1):
+                if step == half - 1 and way != (0 if which == 0 else 1):
+                    continue
+                if step > 0:
+                    previous[(way, which)].wait_recv()
+                    previous.pop((way, which))
+                copy = copy_of(way, step, which)
+                copy.start()
+                started.append(copy)
+                previous[(way, which)] = copy
+        if step == 0:
+            for which in range(3):
+                outs[which][layer] = ins[which][...]
+    for copy in previous.values():
+        copy.wait_recv()
+    for copy in started:
+        copy.wait_send()
+
+
+def gather_column(arrays, depth, plane):
+    half = depth // 2
+    return pl.pallas_call(
+        functools.partial(ring_kernel, depth, plane),
+        out_shape=[jax.ShapeDtypeStruct((depth,) + a.shape, a.dtype) for a in arrays],
+        in_specs=[pl.BlockSpec(memory_space=pltpu.VMEM)] * 3,
+        out_specs=[pl.BlockSpec(memory_space=pltpu.VMEM)] * 3,
+        scratch_shapes=[
+            pltpu.SemaphoreType.DMA((2, half, 3)),
+            pltpu.SemaphoreType.DMA((2, half, 3)),
+        ],
+        compiler_params=pltpu.CompilerParams(
+            collective_id=0, has_side_effects=True, vmem_limit_bytes=16 * 1024 * 1024
+        ),
+    )(*arrays)
 
 
 def to_tiles(matrix):
@@ -102,15 +201,39 @@
             tiled=True,
         ).reshape(expert_count * capacity, model_width)
 
-    select, slot_weight = slot_select(routes, combine, expert_count, capacity)
-    slot_input = jnp.dot(select, layer_input, preferred_element_type=jnp.float32).astype(
-        jnp.bfloat16
-    )
-    slot_input = swap_tokens(slot_input)
+    plane = PLANE
+    depth = expert_count // plane
+    layer = lax.axis_index("expert") // plane
+    groups = [[z * plane + spot for spot in range(plane)] for z in range(depth)]
+
+    def send_in_plane(rows):
+        return lax.all_to_all(
+            rows.reshape(plane, depth * capacity, model_width),
+            "expert",
+            split_axis=0,
+            concat_axis=0,
+            axis_index_groups=groups,
+            tiled=True,
+        ).reshape(expert_count * capacity, model_width)
+
+    notes = jnp.concatenate([routes.T.astype(jnp.float32), combine.T], axis=0)
+    notes = jnp.pad(notes, ((0, 0), (0, LANE - tok_rows)))
+    all_input, all_grad, all_notes = gather_column((layer_input, out_grad, notes), depth, plane)
+    all_notes = all_notes[:, :, :tok_rows].transpose(1, 0, 2).reshape(2 * top_count, -1)
+    column_routes = all_notes[:top_count].astype(jnp.int32)
+    pick, slot_weight = column_select(
+        column_routes, all_notes[top_count:], layer * plane, plane, depth, capacity
+    )
+    slot_input = jnp.dot(
+        pick, all_input.reshape(-1, model_width), preferred_element_type=jnp.float32
+    ).astype(jnp.bfloat16)
+    slot_input = send_in_plane(slot_input)
     slot_grad = (
-        jnp.dot(select, out_grad, preferred_element_type=jnp.float32) * slot_weight[:, None]
+        jnp.dot(pick, all_grad.reshape(-1, model_width), preferred_element_type=jnp.float32)
+        * slot_weight[:, None]
     ).astype(jnp.bfloat16)
-    slot_grad = swap_tokens(slot_grad)
+    slot_grad = send_in_plane(slot_grad)
+    select = home_select(routes, expert_count, capacity)
 
     pre_act = jnp.dot(slot_input, gate_up, preferred_element_type=jnp.float32)
     gate_pre = pre_act[:, :hidden_units]
@@ -128,7 +251,8 @@
         d_pre, gate_up, (((1,), (1,)), ((), ())), preferred_element_type=jnp.float32
     ).astype(jnp.bfloat16)
     slot_back, d_pre, hidden = lax.optimization_barrier((slot_back, d_pre, hidden))
-    returned = swap_tokens(slot_back)
+    by_home = slot_back.reshape(plane, depth, capacity, model_width).transpose(1, 0, 2, 3)
+    returned = swap_tokens(by_home)
 
     grad_down = lax.dot_general(
         hidden, slot_grad, (((0,), (0,)), ((), ())), preferred_element_type=jnp.float32

time: 396 us -> 369 us (0.932)
  waiting for transfers between devices: 283 us -> 225 us
  Pallas kernels: 0 us -> 28.4 us
  starting transfers between devices: 46.8 us -> 42.3 us
    all_to_all x3 -> x1, waiting for transfers between devices: 116 us -> 19.8 us  [swap_tokens(): lax.all_to_all(rows.reshape(expert_count, capacity, model_width), 'expert...]
    all_to_all x0 -> x2, waiting for transfers between devices: none -> 41.5 us  [send_in_plane(): lax.all_to_all(rows.reshape(plane, depth * capacity, model_width), 'exper...]
    pallas_call x0 -> x1, Pallas kernels: none -> 28.4 us  [gather_column(): pl.pallas_call(functools.partial(ring_kernel, depth, plane), out_shape=[j...]
    all_to_all x3 -> x1, starting transfers between devices: 30.6 us -> 11.1 us  [swap_tokens(): lax.all_to_all(rows.reshape(expert_count, capacity, model_width), 'expert...]
    all_to_all x0 -> x2, starting transfers between devices: none -> 14.4 us  [send_in_plane(): lax.all_to_all(rows.reshape(plane, depth * capacity, model_width), 'exper...]
    unnamed x36 -> x37, local copies, waits for them, and re-layouts: 8.49 us -> 8.25 us
  transfers between devices with their start and end apart: 7 -> 7, of which waited for: 6 -> 6; matrix products, arithmetic and copies ran while one was open for 8% -> 9% of each run, Pallas kernels for 0% -> 0%
where the time goes in v3:
time: 369 us; the launch traced here: 368 us
  waiting for transfers between devices  225 us (61%)
  starting transfers between devices  42.3 us (11%)
  Pallas kernels  28.4 us (8%)
  matrix products  26.6 us (7%)
  local copies, waits for them, and re-layouts  22.5 us (6%)
  other arithmetic  16.9 us (5%)
    all_to_all x1, waiting for transfers between devices, per_device(): lax.all_to_all(packed, 'expert', split_axis=0, concat_axis=0, tiled=True)  82 us
    all_to_all x1, waiting for transfers between devices, per_device(): lax.all_to_all(picked, 'expert', split_axis=0, concat_axis=0, tiled=True)  80.2 us
    all_to_all x2, waiting for transfers between devices, send_in_plane(): lax.all_to_all(rows.reshape(plane, depth * capacity, model_width), 'exper...  41.5 us
    pallas_call x1, Pallas kernels, gather_column(): pl.pallas_call(functools.partial(ring_kernel, depth, plane), out_shape=[j...  28.4 us
    all_to_all x1, waiting for transfers between devices, swap_tokens(): lax.all_to_all(rows.reshape(expert_count, capacity, model_width), 'expert...  19.8 us
    all_to_all x2, starting transfers between devices, send_in_plane(): lax.all_to_all(rows.reshape(plane, depth * capacity, model_width), 'exper...  14.4 us
    all_to_all x1, starting transfers between devices, swap_tokens(): lax.all_to_all(rows.reshape(expert_count, capacity, model_width), 'expert...  11.1 us
    all_to_all x1, starting transfers between devices, per_device(): lax.all_to_all(picked, 'expert', split_axis=0, concat_axis=0, tiled=True)  8.77 us
  transfers between devices with their start and end apart: 7, of which 6 were waited for; matrix products, arithmetic and copies ran while one was open for 9% of the time, Pallas kernels for 0%

profile of v3, /device:TPU:2, one launch (start us, length us, event | category | flops | bytes accessed | tf_op | source)
XLA Modules:
  0.0 367.6 jit_solution(18374236793225429532)
XLA Ops:
  0.7 0.7 convert_bitcast_fusion.4
  1.4 0.7 select_maximum_fusion.refs_2_
  2.1 0.9 copy-done
  3.0 0.9 copy-done.1
  3.9 28.4 %shard_map.162 = (bf16[8,64,1024]{2,1,0:T(8,128)(2,1)S(1)}, bf16[8,64,1024]{2,1,0:T(8,128)(2,1)S(1)}, f32[8,16,128]{2,1,0:T(8,128)S(1)}) custom-call(bf16[64,1024]{1,0:T(8,128)(2,1)S(1)} %copy-done, bf16[64,1024]{1,0:T(8,128)(2,1)S(1)} %copy-done.1, f32[16,128]{1,0:T(8,128)S(1)} %select_maximum_fusion.refs_2_), custom_call_target="tpu_custom_call" | custom-call | tf_op jit(solution)/shard_map/pallas_call | solution.py:130
  33.1 2.6 convolution_convert_fusion
  35.7 7.5 %all-to-all-start = ((bf16[16,64,1024]{2,1,0:T(8,128)(2,1)}), bf16[16,64,1024]{2,1,0:T(8,128)(2,1)S(1)}, u32[]{:S(2)}, u32[]{:S(2)}) async-start(bf16[16,64,1024]{2,1,0:T(8,128)(2,1)} %bitcast.168), calls=%async_computation | async-start | bytes 4194304 | tf_op jit(solution)/shard_map/all_to_all | solution.py:210
  43.8 3.7 %multiply_convert_fusion = bf16[1024,1024]{1,0:T(8,128)(2,1)} fusion(pred[1024,512]{1,0:T(32,128)(4,1)} %bitcast.178, bf16[512,1024]{1,0:T(8,128)(2,1)S(1)} %bitcast.157, f32[1024]{0:T(1024)S(1)} %mul.148), kind=kOutput, calls=%fused_computation.1 | convolution fusion | flops 1075838976 | bytes 3674112 | tf_op jit(solution)/shard_map/dot_general | solution.py:232
  47.5 21.5 %all-to-all-done = bf16[16,64,1024]{2,1,0:T(8,128)(2,1)S(1)} async-done(((bf16[16,64,1024]{2,1,0:T(8,128)(2,1)}), bf16[16,64,1024]{2,1,0:T(8,128)(2,1)S(1)}, u32[]{:S(2)}, u32[]{:S(2)}) %all-to-all-start) | async-done | bytes 2097184 | tf_op jit(solution)/shard_map/all_to_all | solution.py:210
  69.0 7.0 %all-to-all-start.1 = ((bf16[16,64,1024]{2,1,0:T(8,128)(2,1)}), bf16[16,64,1024]{2,1,0:T(8,128)(2,1)}, u32[]{:S(2)}, u32[]{:S(2)}) async-start(bf16[16,64,1024]{2,1,0:T(8,128)(2,1)} %bitcast.169), calls=%async_computation.1 | async-start | bytes 4194304 | tf_op jit(solution)/shard_map/all_to_all | solution.py:210
  75.9 5.0 %fusion.5 = f32[1024,768]{0,1:T(8,128)} fusion(bf16[1024,1024]{1,0:T(8,128)(2,1)S(1)} %bitcast.166, bf16[1,1024,768]{2,1,0:T(8,128)(2,1)} %param.15), kind=kOutput, calls=%fused_computation.17 | convolution fusion | flops 1610612736 | bytes 6815744 | tf_op jit(solution)/shard_map/dot_general | solution.py:238
  80.9 20.0 %all-to-all-done.1 = bf16[16,64,1024]{2,1,0:T(8,128)(2,1)} async-done(((bf16[16,64,1024]{2,1,0:T(8,128)(2,1)}), bf16[16,64,1024]{2,1,0:T(8,128)(2,1)}, u32[]{:S(2)}, u32[]{:S(2)}) %all-to-all-start.1) | async-done | bytes 2097184 | tf_op jit(solution)/shard_map/all_to_all | solution.py:210
  100.9 4.9 %multiply_convert_fusion.3 = (bf16[1024,384]{0,1:T(8,128)(2,1)S(1)}, bf16[1024,384]{0,1:T(8,128)(2,1)S(1)}, bf16[1024,384]{0,1:T(8,128)(2,1)}) fusion(f32[1024,768]{0,1:T(8,128)} %fusion.5, bf16[1024,1024]{1,0:T(8,128)(2,1)} %bitcast.13, bf16[1,384,1024]{2,1,0:T(8,128)(2,1)S(1)} %copy-done.10), kind=kOutput, calls=%fused_computation.25 | convolution fusion | flops 811204608 | bytes 8388608 | tf_op jit(solution)/shard_map/dot_general | solution.py:244
  105.8 1.3 pad_maximum_fusion
  107.1 0.7 copy-done.9
  107.8 1.9 convolution_convert_fusion.1
  109.7 1.6 copy.29
  111.3 11.1 %all-to-all-start.2 = ((bf16[128,8,1024]{2,1,0:T(8,128)(2,1)}), bf16[128,8,1024]{2,1,0:T(8,128)(2,1)S(1)}, u32[]{:S(2)}, u32[]{:S(2)}) async-start(bf16[128,8,1024]{2,1,0:T(8,128)(2,1)} %bitcast.160), calls=%async_computation.2 | async-start | bytes 4194304 | tf_op jit(solution)/shard_map/all_to_all | solution.py:196
  122.3 4.0 %fusion.46 = f32[1024,768]{1,0:T(8,128)S(1)} fusion(bf16[1024,1024]{1,0:T(8,128)(2,1)} %bitcast.167, bf16[1024,768]{0,1:T(8,128)(2,1)} %pad_maximum_fusion), kind=kOutput, calls=%fused_computation.109 | convolution fusion | flops 1610612736 | bytes 6815744 | tf_op jit(solution)/shard_map/dot_general | solution.py:260
  126.3 1.1 dynamic-slice_convert_fusion
  127.4 2.8 fusion.47
  130.2 0.9 dynamic-slice_convert_fusion.1
  131.8 1.7 collective-permute-done.1
  133.4 1.8 abs_reduce_fusion.1
  135.3 2.1 abs_reduce_fusion
  138.7 3.0 pmax.7
  142.4 3.9 %fusion.23 = (bf16[512,768]{1,0:T(8,128)(2,1)S(1)}, bf16[512,768]{1,0:T(8,128)(2,1)S(1)}, bf16[512,768]{1,0:T(8,128)(2,1)S(1)}) fusion(f32[]{:T(128)S(6)} %div.36, f32[1,512,768]{2,1,0:T(8,128)} %param.18, bf16[512,768]{1,0:T(8,128)(2,1)S(1)} %collective-permute-done, f32[1024,768]{1,0:T(8,128)} %copy-done.2, s32[]{:T(128)S(6)} %select_n.84, ...), kind=kLoop, calls=%fused_computation.58 | loop fusion | flops 7864320 | bytes 8650760 | tf_op jit(solution)/shard_map/convert_element_type | solution.py:167
  146.4 0.9 constant_dynamic-update-slice_fusion.5
  147.3 0.9 constant_dynamic-update-slice_fusion.4
  148.2 1.0 constant_dynamic-update-slice_fusion.3
  149.2 0.7 fusion.29
  149.9 0.8 constant_dynamic-update-slice_fusion.2
  150.7 0.8 constant_dynamic-update-slice_fusion.1
  151.5 0.8 constant_dynamic-update-slice_fusion
  152.3 0.7 broadcast_dynamic-update-slice_fusion
  153.0 19.8 %all-to-all-done.2 = bf16[128,8,1024]{2,1,0:T(8,128)(2,1)S(1)} async-done(((bf16[128,8,1024]{2,1,0:T(8,128)(2,1)}), bf16[128,8,1024]{2,1,0:T(8,128)(2,1)S(1)}, u32[]{:S(2)}, u32[]{:S(2)}) %all-to-all-start.2) | async-done | bytes 2097184 | tf_op jit(solution)/shard_map/all_to_all | solution.py:196
  172.7 7.7 %all-to-all-start.3 = ((bf16[128,14,8,128]{3,2,1,0:T(8,128)(2,1)}), bf16[128,14,8,128]{3,2,1,0:T(8,128)(2,1)}, u32[]{:S(2)}, u32[]{:S(2)}) async-start(bf16[128,14,8,128]{3,2,1,0:T(8,128)(2,1)} %bitcast.40), calls=%async_computation.3 | async-start | bytes 7340032 | tf_op jit(solution)/shard_map/all_to_all | solution.py:291
  180.7 82.0 %all-to-all-done.3 = bf16[128,14,8,128]{3,2,1,0:T(8,128)(2,1)} async-done(((bf16[128,14,8,128]{3,2,1,0:T(8,128)(2,1)}), bf16[128,14,8,128]{3,2,1,0:T(8,128)(2,1)}, u32[]{:S(2)}, u32[]{:S(2)}) %all-to-all-start.3) | async-done | bytes 3670048 | tf_op jit(solution)/shard_map/all_to_all | solution.py:291
  262.7 4.9 %gather_fusion = bf16[128,14,8,128]{3,2,1,0:T(8,128)(2,1)} fusion(bf16[128,14,8,128]{3,2,1,0:T(8,128)(2,1)} %all-to-all-done.3, s32[1024]{0:T(1024)S(1)} %pad_clamp_fusion), kind=kCustom, calls=%fused_computation | custom fusion | bytes 7340544 | tf_op jit(solution)/shard_map/gather | solution.py:295
  267.5 8.8 %all-to-all-start.4 = ((bf16[128,14,8,128]{3,2,1,0:T(8,128)(2,1)}), bf16[128,14,8,128]{3,2,1,0:T(8,128)(2,1)}, u32[]{:S(2)}, u32[]{:S(2)}) async-start(bf16[128,14,8,128]{3,2,1,0:T(8,128)(2,1)} %gather_fusion), calls=%async_computation.4 | async-start | bytes 7340032 | tf_op jit(solution)/shard_map/all_to_all | solution.py:296
  277.0 1.3 convolution_convert_fusion.2
  278.3 80.2 %all-to-all-done.4 = bf16[128,14,8,128]{3,2,1,0:T(8,128)(2,1)} async-done(((bf16[128,14,8,128]{3,2,1,0:T(8,128)(2,1)}), bf16[128,14,8,128]{3,2,1,0:T(8,128)(2,1)}, u32[]{:S(2)}, u32[]{:S(2)}) %all-to-all-start.4) | async-done | bytes 3670048 | tf_op jit(solution)/shard_map/all_to_all | solution.py:296
  358.5 2.6 fusion.44
  361.1 2.1 fusion.43
  363.2 1.3 convert_bitcast_fusion
  364.4 1.3 convert_bitcast_fusion.1
  365.7 1.0 convert_bitcast_fusion.2
  366.6 1.0 convert_bitcast_fusion.3
  (56 shorter events, 3.0 us)
Async XLA Ops:
  2.1 0.9 copy-start
  3.0 0.9 copy-start.1
  33.1 2.6 copy-start.8
  35.7 33.2 %all-to-all-start = ((bf16[16,64,1024]{2,1,0:T(8,128)(2,1)}), bf16[16,64,1024]{2,1,0:T(8,128)(2,1)S(1)}, u32[]{:S(2)}, u32[]{:S(2)}) async-start(bf16[16,64,1024]{2,1,0:T(8,128)(2,1)} %bitcast.168), calls=%async_computation | async-start | bytes 4194304 | tf_op jit(solution)/shard_map/all_to_all | solution.py:210
  69.0 7.0 %copy-start.5 = (bf16[16,64,1024]{2,1,0:T(8,128)(2,1)}, bf16[16,64,1024]{2,1,0:T(8,128)(2,1)S(1)}, u32[]{:S(2)}) copy-start(bf16[16,64,1024]{2,1,0:T(8,128)(2,1)S(1)} %all-to-all-done) | copy-start | bytes 6291460
  69.0 32.0 %all-to-all-start.1 = ((bf16[16,64,1024]{2,1,0:T(8,128)(2,1)}), bf16[16,64,1024]{2,1,0:T(8,128)(2,1)}, u32[]{:S(2)}, u32[]{:S(2)}) async-start(bf16[16,64,1024]{2,1,0:T(8,128)(2,1)} %bitcast.169), calls=%async_computation.1 | async-start | bytes 4194304 | tf_op jit(solution)/shard_map/all_to_all | solution.py:210
  75.9 25.0 %copy-start.10 = (bf16[1,384,1024]{2,1,0:T(8,128)(2,1)S(1)}, bf16[1,384,1024]{2,1,0:T(8,128)(2,1)}, u32[]{:S(2)}) copy-start(bf16[1,384,1024]{2,1,0:T(8,128)(2,1)} %param.16) | copy-start | bytes 2359300
  105.8 2.0 copy-start.9
  111.3 61.5 %all-to-all-start.2 = ((bf16[128,8,1024]{2,1,0:T(8,128)(2,1)}), bf16[128,8,1024]{2,1,0:T(8,128)(2,1)S(1)}, u32[]{:S(2)}, u32[]{:S(2)}) async-start(bf16[128,8,1024]{2,1,0:T(8,128)(2,1)} %bitcast.160), calls=%async_computation.2 | async-start | bytes 4194304 | tf_op jit(solution)/shard_map/all_to_all | solution.py:196
  122.3 5.1 %copy-start.14 = (bf16[1024,384]{0,1:T(8,128)(2,1)S(1)}, bf16[1024,384]{0,1:T(8,128)(2,1)}, u32[]{:S(2)}) copy-start(bf16[1024,384]{0,1:T(8,128)(2,1)} %get-tuple-element.19) | copy-start | bytes 2359300
  126.3 3.9 %copy-start.2 = (f32[1024,768]{1,0:T(8,128)}, f32[1024,768]{1,0:T(8,128)S(1)}, u32[]{:S(2)}) copy-start(f32[1024,768]{1,0:T(8,128)S(1)} %fusion.46) | copy-start | bytes 9437188
  127.4 7.9 %collective-permute-start = (bf16[512,768]{1,0:T(8,128)(2,1)}, bf16[512,768]{1,0:T(8,128)(2,1)S(1)}, u32[]{:S(2)}, u32[]{:S(2)}) collective-permute-start(bf16[512,768]{1,0:T(8,128)(2,1)} %dynamic-slice_convert_fusion), channel_id=1, source_target_pairs={{0,128},{128,0},{1,129},{129,1},{2,130},{130,2},{3,131},{131,3},{4... | collective-permute-start | bytes 2359304 | tf_op jit(solution)/shard_map/ppermute | solution.py:269
  130.2 1.3 copy-start.3
  131.5 1.9 collective-permute-start.1
  146.3 2.9 copy-start.4
  146.3 2.9 copy-start.6
  146.3 2.9 copy-start.7
  146.4 2.8 copy-start.11
  172.7 7.7 %copy-start.13 = (s32[32,2]{0,1:T(2,128)S(1)}, s32[32,2]{0,1:T(2,128)}, u32[]{:S(2)}) copy-start(s32[32,2]{0,1:T(2,128)} %param.21) | copy-start | bytes 772
  172.7 89.9 %all-to-all-start.3 = ((bf16[128,14,8,128]{3,2,1,0:T(8,128)(2,1)}), bf16[128,14,8,128]{3,2,1,0:T(8,128)(2,1)}, u32[]{:S(2)}, u32[]{:S(2)}) async-start(bf16[128,14,8,128]{3,2,1,0:T(8,128)(2,1)} %bitcast.40), calls=%async_computation.3 | async-start | bytes 7340032 | tf_op jit(solution)/shard_map/all_to_all | solution.py:291
  267.5 8.8 %copy-start.12 = (s32[64,8]{0,1:T(8,128)S(1)}, s32[64,8]{0,1:T(8,128)}, u32[]{:S(2)}) copy-start(s32[64,8]{0,1:T(8,128)} %param.14) | copy-start | bytes 6148
  267.5 90.9 %all-to-all-start.4 = ((bf16[128,14,8,128]{3,2,1,0:T(8,128)(2,1)}), bf16[128,14,8,128]{3,2,1,0:T(8,128)(2,1)}, u32[]{:S(2)}, u32[]{:S(2)}) async-start(bf16[128,14,8,128]{3,2,1,0:T(8,128)(2,1)} %gather_fusion), calls=%async_computation.4 | async-start | bytes 7340032 | tf_op jit(solution)/shard_map/all_to_all | solution.py:296

commit v4 on v3

--- a/solution.py
+++ b/solution.py
@@ -67,10 +67,10 @@
     return select, slot_weight.reshape(-1)
 
 
-def ring_kernel(depth, plane, *refs):
-    ins = refs[:3]
-    outs = refs[3:6]
-    send_sem, recv_sem = refs[6:]
+def ring_kernel(depth, plane, count, *refs):
+    ins = refs[:count]
+    outs = refs[count : 2 * count]
+    send_sem, recv_sem = refs[2 * count :]
     me = lax.axis_index("expert")
     layer = me // plane
     spot = me % plane
@@ -93,9 +93,14 @@
         else:
             block = (layer + step) % depth
         source = ins[which] if step == 0 else outs[which].at[block]
+        target = outs[which].at[block]
+        if step == half - 1:
+            rows = ins[which].shape[0] // 2
+            source = source.at[pl.ds(way * rows, rows)]
+            target = target.at[pl.ds(way * rows, rows)]
         return pltpu.make_async_remote_copy(
             src_ref=source,
-            dst_ref=outs[which].at[block],
+            dst_ref=target,
             send_sem=send_sem.at[way, step, which],
             recv_sem=recv_sem.at[way, step, which],
             device_id={"expert": targets[way]},
@@ -105,19 +110,16 @@
     started = []
     previous = {}
     for step in range(half):
-        for which in (2, 0, 1):
+        for which in range(count):
             for way in (0, 1):
-                if step == half - 1 and way != (0 if which == 0 else 1):
-                    continue
                 if step > 0:
                     previous[(way, which)].wait_recv()
-                    previous.pop((way, which))
                 copy = copy_of(way, step, which)
                 copy.start()
                 started.append(copy)
                 previous[(way, which)] = copy
         if step == 0:
-            for which in range(3):
+            for which in range(count):
                 outs[which][layer] = ins[which][...]
     for copy in previous.values():
         copy.wait_recv()
@@ -125,33 +127,67 @@
         copy.wait_send()
 
 
-def gather_column(arrays, depth, plane):
+def gather_column(arrays, depth, plane, collective_id):
     half = depth // 2
+    count = len(arrays)
+    moved = sum(a.size * a.dtype.itemsize for a in arrays) * depth
     return pl.pallas_call(
-        functools.partial(ring_kernel, depth, plane),
+        functools.partial(ring_kernel, depth, plane, count),
         out_shape=[jax.ShapeDtypeStruct((depth,) + a.shape, a.dtype) for a in arrays],
-        in_specs=[pl.BlockSpec(memory_space=pltpu.VMEM)] * 3,
-        out_specs=[pl.BlockSpec(memory_space=pltpu.VMEM)] * 3,
+        in_specs=[pl.BlockSpec(memory_space=pltpu.VMEM)] * count,
+        out_specs=[pl.BlockSpec(memory_space=pltpu.VMEM)] * count,
         scratch_shapes=[
-            pltpu.SemaphoreType.DMA((2, half, 3)),
-            pltpu.SemaphoreType.DMA((2, half, 3)),
+            pltpu.SemaphoreType.DMA((2, half, count)),
+            pltpu.SemaphoreType.DMA((2, half, count)),
         ],
         compiler_params=pltpu.CompilerParams(
-            collective_id=0, has_side_effects=True, vmem_limit_bytes=16 * 1024 * 1024
+            collective_id=collective_id,
+            has_side_effects=True,
+            vmem_limit_bytes=16 * 1024 * 1024,
         ),
+        cost_estimate=pl.CostEstimate(flops=0, bytes_accessed=40 * moved, transcendentals=0),
     )(*arrays)
+
+
+UNPACK_STEPS = 8
+
+
+def unpack_kernel(*refs):
+    for tiles, out in zip(refs[:6], refs[6:]):
+        cols = out.shape[1] // LANE
+        for group in range(out.shape[0] // SUB):
+            for col in range(cols):
+                out[group * SUB : (group + 1) * SUB, col * LANE : (col + 1) * LANE] = tiles[
+                    group * cols + col
+                ].astype(out.dtype)
+
+
+def unpack_tiles(arrived, shapes, dtypes):
+    in_specs = []
+    out_specs = []
+    start = 0
+    for rows, cols in shapes:
+        count = rows * cols // (SUB * LANE)
+        block = count // UNPACK_STEPS
+        first = start // block
+        in_specs.append(
+            pl.BlockSpec((block, SUB, LANE), functools.partial(lambda b, i: (b + i, 0, 0), first))
+        )
+        out_specs.append(pl.BlockSpec((rows // UNPACK_STEPS, cols), lambda i: (i, 0)))
+        start += count
+    return pl.pallas_call(
+        unpack_kernel,
+        grid=(UNPACK_STEPS,),
+        out_shape=[jax.ShapeDtypeStruct(s, d) for s, d in zip(shapes, dtypes)],
+        in_specs=in_specs,
+        out_specs=out_specs,
+    )(*([arrived] * 6))
 
 
 def to_tiles(matrix):
     rows, cols = matrix.shape
     tiles = matrix.reshape(rows // SUB, SUB, cols // LANE, LANE).transpose(0, 2, 1, 3)
     return tiles.reshape(-1, SUB, LANE)
-
-
-def from_tiles(tiles, rows, cols):
-    return (
-        tiles.reshape(rows // SUB, cols // LANE, SUB, LANE).transpose(0, 2, 1, 3).reshape(rows, cols)
-    )
 
 
 def adam_update(weight, grad, mean_in, square_in, scale_by):
@@ -218,7 +254,7 @@
 
     notes = jnp.concatenate([routes.T.astype(jnp.float32), combine.T], axis=0)
     notes = jnp.pad(notes, ((0, 0), (0, LANE - tok_rows)))
-    all_input, all_grad, all_notes = gather_column((layer_input, out_grad, notes), depth, plane)
+    all_notes, all_input = gather_column((notes, layer_input), depth, plane, 0)
     all_notes = all_notes[:, :, :tok_rows].transpose(1, 0, 2).reshape(2 * top_count, -1)
     column_routes = all_notes[:top_count].astype(jnp.int32)
     pick, slot_weight = column_select(
@@ -227,7 +263,9 @@
     slot_input = jnp.dot(
         pick, all_input.reshape(-1, model_width), preferred_element_type=jnp.float32
     ).astype(jnp.bfloat16)
+    slot_input, out_grad = lax.optimization_barrier((slot_input, out_grad))
     slot_input = send_in_plane(slot_input)
+    (all_grad,) = gather_column((out_grad,), depth, plane, 1)
     slot_grad = (
         jnp.dot(pick, all_grad.reshape(-1, model_width), preferred_element_type=jnp.float32)
         * slot_weight[:, None]
@@ -295,20 +333,18 @@
     picked = spread.at[partner].get(mode="promise_in_bounds")
     arrived = lax.all_to_all(picked, "expert", split_axis=0, concat_axis=0, tiled=True)
     arrived = arrived.reshape(-1, SUB, LANE)
-    moved = []
-    start = 0
-    for u, count in zip(updated, counts):
-        moved.append(from_tiles(arrived[start : start + count], *u.shape))
-        start += count
-    new_gu, gate_mean, gate_square, new_dn, down_mean, down_square = moved
+    wide = (jnp.bfloat16, jnp.float32, jnp.float32)
+    new_gu, gate_mean, gate_square, new_dn, down_mean, down_square = unpack_tiles(
+        arrived, [u.shape for u in updated], wide + wide
+    )
     return (
         in_grad,
         new_gu[None],
         new_dn[None],
-        gate_mean.astype(jnp.float32)[None],
-        gate_square.astype(jnp.float32)[None],
-        down_mean.astype(jnp.float32)[None],
-        down_square.astype(jnp.float32)[None],
+        gate_mean[None],
+        gate_square[None],
+        down_mean[None],
+        down_square[None],
     )
 
 

time: 369 us -> 357 us (0.967)
  waiting for transfers between devices: 225 us -> 201 us
  Pallas kernels: 28.4 us -> 51.4 us
  local copies, waits for them, and re-layouts: 22.5 us -> 16.8 us
  other arithmetic: 16.9 us -> 12.5 us
    all_to_all x2, waiting for transfers between devices: 41.5 us -> 17.4 us  [send_in_plane(): lax.all_to_all(rows.reshape(plane, depth * capacity, model_width), 'exper...]
    pallas_call x1 -> x3, Pallas kernels: 28.4 us -> 51.4 us  [the longest x2 44.8 us: gather_column(): pl.pallas_call(functools.partial(ring_kernel, depth, plane, count), out_s...]
    slice x2 -> x0, local copies, waits for them, and re-layouts: 4.69 us -> none  [per_device(): moved.append(from_tiles(arrived[start:start + count], *u.shape))]
    convert_element_type x4 -> x0, other arithmetic: 4.45 us -> none  [the longest x1 1.25 us: per_device(): gate_square.astype(jnp.float32)[None]]
    unnamed x37 -> x35, local copies, waits for them, and re-layouts: 8.25 us -> 7.32 us
  transfers between devices with their start and end apart: 7 -> 7, of which waited for: 6 -> 5; matrix products, arithmetic and copies ran while one was open for 9% -> 9% of each run, Pallas kernels for 0% -> 6%
where the time goes in v4:
time: 357 us; the launch traced here: 356 us
  waiting for transfers between devices  201 us (56%)
  Pallas kernels  51.4 us (14%)
  starting transfers between devices  43.1 us (12%)
  matrix products  25.6 us (7%)
  local copies, waits for them, and re-layouts  16.8 us (5%)
  other arithmetic  12.5 us (4%)
    all_to_all x1, waiting for transfers between devices, per_device(): lax.all_to_all(packed, 'expert', split_axis=0, concat_axis=0, tiled=True)  81.9 us
    all_to_all x1, waiting for transfers between devices, per_device(): lax.all_to_all(picked, 'expert', split_axis=0, concat_axis=0, tiled=True)  80 us
    pallas_call x2, Pallas kernels, gather_column(): pl.pallas_call(functools.partial(ring_kernel, depth, plane, count), out_s...  44.8 us
    all_to_all x1, waiting for transfers between devices, swap_tokens(): lax.all_to_all(rows.reshape(expert_count, capacity, model_width), 'expert...  19.7 us
    all_to_all x2, waiting for transfers between devices, send_in_plane(): lax.all_to_all(rows.reshape(plane, depth * capacity, model_width), 'exper...  17.4 us
    all_to_all x2, starting transfers between devices, send_in_plane(): lax.all_to_all(rows.reshape(plane, depth * capacity, model_width), 'exper...  14.5 us
    all_to_all x1, starting transfers between devices, swap_tokens(): lax.all_to_all(rows.reshape(expert_count, capacity, model_width), 'expert...  11.8 us
    all_to_all x1, starting transfers between devices, per_device(): lax.all_to_all(picked, 'expert', split_axis=0, concat_axis=0, tiled=True)  8.78 us
  transfers between devices with their start and end apart: 7, of which 5 were waited for; matrix products, arithmetic and copies ran while one was open for 9% of the time, Pallas kernels for 6%

profile of v4, /device:TPU:2, one launch (start us, length us, event | category | flops | bytes accessed | tf_op | source)
XLA Modules:
  0.0 356.3 jit_solution(3635756798409918544)
XLA Ops:
  0.7 0.7 convert_bitcast_fusion
  1.4 0.7 select_maximum_fusion.refs_0_
  2.1 0.9 copy-done.1
  3.0 22.5 %shard_map.162 = (f32[8,16,128]{2,1,0:T(8,128)S(1)}, bf16[8,64,1024]{2,1,0:T(8,128)(2,1)S(1)}) custom-call(f32[16,128]{1,0:T(8,128)S(1)} %select_maximum_fusion.refs_0_, bf16[64,1024]{1,0:T(8,128)(2,1)S(1)} %copy-done.1), custom_call_target="tpu_custom_call" | custom-call | bytes 44564480 | tf_op jit(solution)/shard_map/pallas_call | solution.py:134
  25.7 0.3 fusion.9
  26.0 0.3 iota_compare_fusion
  26.4 2.6 convolution_convert_fusion
  29.0 7.6 %all-to-all-start = ((bf16[16,64,1024]{2,1,0:T(8,128)(2,1)}), bf16[16,64,1024]{2,1,0:T(8,128)(2,1)S(1)}, u32[]{:S(2)}, u32[]{:S(2)}) async-start(bf16[16,64,1024]{2,1,0:T(8,128)(2,1)} %bitcast.138), calls=%async_computation | async-start | bytes 4194304 | tf_op jit(solution)/shard_map/all_to_all | solution.py:246
  36.8 0.3 select_reduce_fusion
  37.1 22.3 %shard_map.163 = bf16[8,64,1024]{2,1,0:T(8,128)(2,1)S(1)} custom-call(bf16[64,1024]{1,0:T(8,128)(2,1)S(1)} %copy-done), custom_call_target="tpu_custom_call" | custom-call | bytes 41943040 | tf_op jit(solution)/shard_map/pallas_call | solution.py:134
  59.4 2.6 multiply_convert_fusion
  62.1 6.9 %all-to-all-start.1 = ((bf16[16,64,1024]{2,1,0:T(8,128)(2,1)}), bf16[16,64,1024]{2,1,0:T(8,128)(2,1)}, u32[]{:S(2)}, u32[]{:S(2)}) async-start(bf16[16,64,1024]{2,1,0:T(8,128)(2,1)} %bitcast.139), calls=%async_computation.1 | async-start | bytes 4194304 | tf_op jit(solution)/shard_map/all_to_all | solution.py:246
  69.0 5.0 %fusion.5 = f32[1024,768]{0,1:T(8,128)} fusion(bf16[1024,1024]{1,0:T(8,128)(2,1)S(1)} %bitcast.136, bf16[1,1024,768]{2,1,0:T(8,128)(2,1)} %param.15), kind=kOutput, calls=%fused_computation.15 | convolution fusion | flops 1610612736 | bytes 6815744 | tf_op jit(solution)/shard_map/dot_general | solution.py:276
  74.0 17.4 %all-to-all-done.1 = bf16[16,64,1024]{2,1,0:T(8,128)(2,1)} async-done(((bf16[16,64,1024]{2,1,0:T(8,128)(2,1)}), bf16[16,64,1024]{2,1,0:T(8,128)(2,1)}, u32[]{:S(2)}, u32[]{:S(2)}) %all-to-all-start.1) | async-done | bytes 2097184 | tf_op jit(solution)/shard_map/all_to_all | solution.py:246
  91.4 4.9 %multiply_convert_fusion.3 = (bf16[1024,384]{0,1:T(8,128)(2,1)S(1)}, bf16[1024,384]{0,1:T(8,128)(2,1)S(1)}, bf16[1024,384]{0,1:T(8,128)(2,1)}) fusion(f32[1024,768]{0,1:T(8,128)} %fusion.5, bf16[1024,1024]{1,0:T(8,128)(2,1)} %bitcast.13, bf16[1,384,1024]{2,1,0:T(8,128)(2,1)S(1)} %copy-done.9), kind=kOutput, calls=%fused_computation.23 | convolution fusion | flops 811204608 | bytes 8388608 | tf_op jit(solution)/shard_map/dot_general | solution.py:282
  96.4 1.3 pad_maximum_fusion
  97.6 0.7 copy-done.8
  98.3 1.9 convolution_convert_fusion.1
  100.2 1.6 copy.29
  101.8 11.8 %all-to-all-start.2 = ((bf16[128,8,1024]{2,1,0:T(8,128)(2,1)}), bf16[128,8,1024]{2,1,0:T(8,128)(2,1)S(1)}, u32[]{:S(2)}, u32[]{:S(2)}) async-start(bf16[128,8,1024]{2,1,0:T(8,128)(2,1)} %bitcast.132), calls=%async_computation.2 | async-start | bytes 4194304 | tf_op jit(solution)/shard_map/all_to_all | solution.py:232
  113.6 4.0 %fusion.44 = f32[1024,768]{1,0:T(8,128)S(1)} fusion(bf16[1024,1024]{1,0:T(8,128)(2,1)} %bitcast.137, bf16[1024,768]{0,1:T(8,128)(2,1)} %pad_maximum_fusion), kind=kOutput, calls=%fused_computation.103 | convolution fusion | flops 1610612736 | bytes 6815744 | tf_op jit(solution)/shard_map/dot_general | solution.py:298
  117.6 1.1 dynamic-slice_convert_fusion
  118.7 2.8 fusion.45
  121.5 0.9 dynamic-slice_convert_fusion.1
  122.4 0.4 copy-done.3
  122.8 0.3 collective-permute-start.1
  123.0 1.7 collective-permute-done.1
  124.7 1.8 abs_reduce_fusion.1
  126.5 2.1 abs_reduce_fusion
  130.0 3.0 pmax.7
  133.6 3.9 %fusion.23 = (bf16[512,768]{1,0:T(8,128)(2,1)S(1)}, bf16[512,768]{1,0:T(8,128)(2,1)S(1)}, bf16[512,768]{1,0:T(8,128)(2,1)S(1)}) fusion(f32[]{:T(128)S(6)} %div.36, f32[1,512,768]{2,1,0:T(8,128)} %param.18, bf16[512,768]{1,0:T(8,128)(2,1)S(1)} %collective-permute-done, f32[1024,768]{1,0:T(8,128)} %copy-done.2, s32[]{:T(128)S(6)} %select_n.84, ...), kind=kLoop, calls=%fused_computation.54 | loop fusion | flops 7864320 | bytes 8650760 | tf_op jit(solution)/shard_map/convert_element_type | solution.py:203
  137.6 0.9 constant_dynamic-update-slice_fusion.5
  138.6 0.9 constant_dynamic-update-slice_fusion.4
  139.5 1.0 constant_dynamic-update-slice_fusion.3
  140.5 0.7 fusion.29
  141.2 0.8 constant_dynamic-update-slice_fusion.2
  142.0 0.8 constant_dynamic-update-slice_fusion.1
  142.8 0.8 constant_dynamic-update-slice_fusion
  143.5 0.7 broadcast_dynamic-update-slice_fusion
  144.2 19.7 %all-to-all-done.2 = bf16[128,8,1024]{2,1,0:T(8,128)(2,1)S(1)} async-done(((bf16[128,8,1024]{2,1,0:T(8,128)(2,1)}), bf16[128,8,1024]{2,1,0:T(8,128)(2,1)S(1)}, u32[]{:S(2)}, u32[]{:S(2)}) %all-to-all-start.2) | async-done | bytes 2097184 | tf_op jit(solution)/shard_map/all_to_all | solution.py:232
  164.0 7.7 %all-to-all-start.3 = ((bf16[128,14,8,128]{3,2,1,0:T(8,128)(2,1)}), bf16[128,14,8,128]{3,2,1,0:T(8,128)(2,1)}, u32[]{:S(2)}, u32[]{:S(2)}) async-start(bf16[128,14,8,128]{3,2,1,0:T(8,128)(2,1)} %bitcast.40), calls=%async_computation.3 | async-start | bytes 7340032 | tf_op jit(solution)/shard_map/all_to_all | solution.py:329
  171.9 81.9 %all-to-all-done.3 = bf16[128,14,8,128]{3,2,1,0:T(8,128)(2,1)} async-done(((bf16[128,14,8,128]{3,2,1,0:T(8,128)(2,1)}), bf16[128,14,8,128]{3,2,1,0:T(8,128)(2,1)}, u32[]{:S(2)}, u32[]{:S(2)}) %all-to-all-start.3) | async-done | bytes 3670048 | tf_op jit(solution)/shard_map/all_to_all | solution.py:329
  253.8 4.9 %gather_fusion = bf16[128,14,8,128]{3,2,1,0:T(8,128)(2,1)} fusion(bf16[128,14,8,128]{3,2,1,0:T(8,128)(2,1)} %all-to-all-done.3, s32[1024]{0:T(1024)S(1)} %pad_clamp_fusion), kind=kCustom, calls=%fused_computation | custom fusion | bytes 7340544 | tf_op jit(solution)/shard_map/gather | solution.py:333
  258.7 8.8 %all-to-all-start.4 = ((bf16[128,14,8,128]{3,2,1,0:T(8,128)(2,1)}), bf16[128,14,8,128]{3,2,1,0:T(8,128)(2,1)}, u32[]{:S(2)}, u32[]{:S(2)}) async-start(bf16[128,14,8,128]{3,2,1,0:T(8,128)(2,1)} %gather_fusion), calls=%async_computation.4 | async-start | bytes 7340032 | tf_op jit(solution)/shard_map/all_to_all | solution.py:334
  267.8 0.2 fusion.10
  268.2 1.3 convolution_convert_fusion.2
  269.5 80.0 %all-to-all-done.4 = bf16[128,14,8,128]{3,2,1,0:T(8,128)(2,1)} async-done(((bf16[128,14,8,128]{3,2,1,0:T(8,128)(2,1)}), bf16[128,14,8,128]{3,2,1,0:T(8,128)(2,1)}, u32[]{:S(2)}, u32[]{:S(2)}) %all-to-all-start.4) | async-done | bytes 3670048 | tf_op jit(solution)/shard_map/all_to_all | solution.py:334
  349.5 6.6 %shard_map.164 = (bf16[512,768]{1,0:T(8,128)(2,1)}, f32[512,768]{1,0:T(8,128)}, f32[512,768]{1,0:T(8,128)}, bf16[384,512]{1,0:T(8,128)(2,1)}, f32[384,512]{1,0:T(8,128)}, /*index=5*/f32[384,512]{1,0:T(8,128)}) custom-call(bf16[1792,8,128]{2,1,0:T(8,128)(2,1)} %bitcast.50.refs_0_.refs_1_.refs_2_.refs_3_.refs_4_.refs_5_, ...), custom_call_target="tpu_custom_call" | custom-call | tf_op jit(solution)/shard_map/pallas_call | solution.py:178
  (50 shorter events, 1.2 us)
Async XLA Ops:
  2.1 0.9 copy-start.1
  29.0 8.2 %copy-start = (bf16[64,1024]{1,0:T(8,128)(2,1)S(1)}, bf16[64,1024]{1,0:T(8,128)(2,1)}, u32[]{:S(2)}) copy-start(bf16[64,1024]{1,0:T(8,128)(2,1)} %refs_0_) | copy-start | bytes 393220
  29.0 33.1 %all-to-all-start = ((bf16[16,64,1024]{2,1,0:T(8,128)(2,1)}), bf16[16,64,1024]{2,1,0:T(8,128)(2,1)S(1)}, u32[]{:S(2)}, u32[]{:S(2)}) async-start(bf16[16,64,1024]{2,1,0:T(8,128)(2,1)} %bitcast.138), calls=%async_computation | async-start | bytes 4194304 | tf_op jit(solution)/shard_map/all_to_all | solution.py:246
  62.1 6.9 %copy-start.5 = (bf16[16,64,1024]{2,1,0:T(8,128)(2,1)}, bf16[16,64,1024]{2,1,0:T(8,128)(2,1)S(1)}, u32[]{:S(2)}) copy-start(bf16[16,64,1024]{2,1,0:T(8,128)(2,1)S(1)} %all-to-all-done) | copy-start | bytes 6291460
  62.1 29.4 %all-to-all-start.1 = ((bf16[16,64,1024]{2,1,0:T(8,128)(2,1)}), bf16[16,64,1024]{2,1,0:T(8,128)(2,1)}, u32[]{:S(2)}, u32[]{:S(2)}) async-start(bf16[16,64,1024]{2,1,0:T(8,128)(2,1)} %bitcast.139), calls=%async_computation.1 | async-start | bytes 4194304 | tf_op jit(solution)/shard_map/all_to_all | solution.py:246
  69.0 22.4 %copy-start.9 = (bf16[1,384,1024]{2,1,0:T(8,128)(2,1)S(1)}, bf16[1,384,1024]{2,1,0:T(8,128)(2,1)}, u32[]{:S(2)}) copy-start(bf16[1,384,1024]{2,1,0:T(8,128)(2,1)} %param.16) | copy-start | bytes 2359300
  96.3 2.0 copy-start.8
  101.8 62.2 %all-to-all-start.2 = ((bf16[128,8,1024]{2,1,0:T(8,128)(2,1)}), bf16[128,8,1024]{2,1,0:T(8,128)(2,1)S(1)}, u32[]{:S(2)}, u32[]{:S(2)}) async-start(bf16[128,8,1024]{2,1,0:T(8,128)(2,1)} %bitcast.132), calls=%async_computation.2 | async-start | bytes 4194304 | tf_op jit(solution)/shard_map/all_to_all | solution.py:232
  113.6 5.1 %copy-start.13 = (bf16[1024,384]{0,1:T(8,128)(2,1)S(1)}, bf16[1024,384]{0,1:T(8,128)(2,1)}, u32[]{:S(2)}) copy-start(bf16[1024,384]{0,1:T(8,128)(2,1)} %get-tuple-element.27) | copy-start | bytes 2359300
  117.6 3.9 %copy-start.2 = (f32[1024,768]{1,0:T(8,128)}, f32[1024,768]{1,0:T(8,128)S(1)}, u32[]{:S(2)}) copy-start(f32[1024,768]{1,0:T(8,128)S(1)} %fusion.44) | copy-start | bytes 9437188
  118.7 7.9 %collective-permute-start = (bf16[512,768]{1,0:T(8,128)(2,1)}, bf16[512,768]{1,0:T(8,128)(2,1)S(1)}, u32[]{:S(2)}, u32[]{:S(2)}) collective-permute-start(bf16[512,768]{1,0:T(8,128)(2,1)} %dynamic-slice_convert_fusion), channel_id=1, source_target_pairs={{0,128},{128,0},{1,129},{129,1},{2,130},{130,2},{3,131},{131,3},{4... | collective-permute-start | bytes 2359304 | tf_op jit(solution)/shard_map/ppermute | solution.py:307
  121.5 1.3 copy-start.3
  122.8 1.9 collective-permute-start.1
  137.6 2.9 copy-start.4
  137.6 2.9 copy-start.6
  137.6 2.9 copy-start.7
  137.6 2.8 copy-start.10
  164.0 7.7 %copy-start.12 = (s32[32,2]{0,1:T(2,128)S(1)}, s32[32,2]{0,1:T(2,128)}, u32[]{:S(2)}) copy-start(s32[32,2]{0,1:T(2,128)} %param.21) | copy-start | bytes 772
  164.0 89.9 %all-to-all-start.3 = ((bf16[128,14,8,128]{3,2,1,0:T(8,128)(2,1)}), bf16[128,14,8,128]{3,2,1,0:T(8,128)(2,1)}, u32[]{:S(2)}, u32[]{:S(2)}) async-start(bf16[128,14,8,128]{3,2,1,0:T(8,128)(2,1)} %bitcast.40), calls=%async_computation.3 | async-start | bytes 7340032 | tf_op jit(solution)/shard_map/all_to_all | solution.py:329
  258.7 8.8 %copy-start.11 = (s32[64,8]{0,1:T(8,128)S(1)}, s32[64,8]{0,1:T(8,128)}, u32[]{:S(2)}) copy-start(s32[64,8]{0,1:T(8,128)} %param.14) | copy-start | bytes 6148
  258.7 90.8 %all-to-all-start.4 = ((bf16[128,14,8,128]{3,2,1,0:T(8,128)(2,1)}), bf16[128,14,8,128]{3,2,1,0:T(8,128)(2,1)}, u32[]{:S(2)}, u32[]{:S(2)}) async-start(bf16[128,14,8,128]{3,2,1,0:T(8,128)(2,1)} %gather_fusion), calls=%async_computation.4 | async-start | bytes 7340032 | tf_op jit(solution)/shard_map/all_to_all | solution.py:334

commit v5 on v4

--- a/solution.py
+++ b/solution.py
@@ -87,22 +87,19 @@
 
     half = depth // 2
 
-    def copy_of(way, step, which):
+    def copy_of(way, step, which, part):
         if way == 0:
             block = (layer + depth - step) % depth
         else:
             block = (layer + step) % depth
-        source = ins[which] if step == 0 else outs[which].at[block]
-        target = outs[which].at[block]
-        if step == half - 1:
-            rows = ins[which].shape[0] // 2
-            source = source.at[pl.ds(way * rows, rows)]
-            target = target.at[pl.ds(way * rows, rows)]
+        rows = ins[which].shape[0] // 2
+        some = pl.ds(part * rows, rows)
+        source = ins[which].at[some] if step == 0 else outs[which].at[block, some]
         return pltpu.make_async_remote_copy(
             src_ref=source,
-            dst_ref=target,
-            send_sem=send_sem.at[way, step, which],
-            recv_sem=recv_sem.at[way, step, which],
+            dst_ref=outs[which].at[block, some],
+            send_sem=send_sem.at[way, step, which, part],
+            recv_sem=recv_sem.at[way, step, which, part],
             device_id={"expert": targets[way]},
             device_id_type=pl.DeviceIdType.MESH,
         )
@@ -111,13 +108,16 @@
     previous = {}
     for step in range(half):
         for which in range(count):
-            for way in (0, 1):
-                if step > 0:
-                    previous[(way, which)].wait_recv()
-                copy = copy_of(way, step, which)
-                copy.start()
-                started.append(copy)
-                previous[(way, which)] = copy
+            for part in (0, 1):
+                for way in (0, 1):
+                    if step == half - 1 and way != part:
+                        continue
+                    if step > 0:
+                        previous.pop((way, which, part)).wait_recv()
+                    copy = copy_of(way, step, which, part)
+                    copy.start()
+                    started.append(copy)
+                    previous[(way, which, part)] = copy
         if step == 0:
             for which in range(count):
                 outs[which][layer] = ins[which][...]
@@ -137,8 +137,8 @@
         in_specs=[pl.BlockSpec(memory_space=pltpu.VMEM)] * count,
         out_specs=[pl.BlockSpec(memory_space=pltpu.VMEM)] * count,
         scratch_shapes=[
-            pltpu.SemaphoreType.DMA((2, half, count)),
-            pltpu.SemaphoreType.DMA((2, half, count)),
+            pltpu.SemaphoreType.DMA((2, half, count, 2)),
+            pltpu.SemaphoreType.DMA((2, half, count, 2)),
         ],
         compiler_params=pltpu.CompilerParams(
             collective_id=collective_id,

time: 357 us -> 357 us (level)
  Pallas kernels: 51.4 us -> 47.8 us
    pallas_call x2, Pallas kernels: 44.8 us -> 41.2 us  [gather_column(): pl.pallas_call(functools.partial(ring_kernel, depth, plane, count), out_s...]
  transfers between devices with their start and end apart: 7 -> 7, of which waited for: 5 -> 6; matrix products, arithmetic and copies ran while one was open for 9% -> 9% of each run, Pallas kernels for 6% -> 5%
where the time goes in v5:
time: 357 us; the launch traced here: 356 us
  waiting for transfers between devices  204 us (57%)
  Pallas kernels  47.8 us (13%)
  starting transfers between devices  43.6 us (12%)
  matrix products  25.6 us (7%)
  local copies, waits for them, and re-layouts  16.8 us (5%)
  other arithmetic  12.5 us (4%)
    all_to_all x1, waiting for transfers between devices, per_device(): lax.all_to_all(packed, 'expert', split_axis=0, concat_axis=0, tiled=True)  81.8 us
    all_to_all x1, waiting for transfers between devices, per_device(): lax.all_to_all(picked, 'expert', split_axis=0, concat_axis=0, tiled=True)  80.1 us
    pallas_call x2, Pallas kernels, gather_column(): pl.pallas_call(functools.partial(ring_kernel, depth, plane, count), out_s...  41.2 us
    all_to_all x2, waiting for transfers between devices, send_in_plane(): lax.all_to_all(rows.reshape(plane, depth * capacity, model_width), 'exper...  21 us
    all_to_all x1, waiting for transfers between devices, swap_tokens(): lax.all_to_all(rows.reshape(expert_count, capacity, model_width), 'expert...  19.6 us
    all_to_all x2, starting transfers between devices, send_in_plane(): lax.all_to_all(rows.reshape(plane, depth * capacity, model_width), 'exper...  14.3 us
    all_to_all x1, starting transfers between devices, swap_tokens(): lax.all_to_all(rows.reshape(expert_count, capacity, model_width), 'expert...  12.5 us
    all_to_all x1, starting transfers between devices, per_device(): lax.all_to_all(picked, 'expert', split_axis=0, concat_axis=0, tiled=True)  8.78 us
  transfers between devices with their start and end apart: 7, of which 6 were waited for; matrix products, arithmetic and copies ran while one was open for 9% of the time, Pallas kernels for 5%

profile of v5, /device:TPU:2, one launch (start us, length us, event | category | flops | bytes accessed | tf_op | source)
XLA Modules:
  0.0 356.4 jit_solution(12591482290549519018)
XLA Ops:
  0.7 0.7 convert_bitcast_fusion
  1.4 0.7 select_maximum_fusion.refs_0_
  2.1 0.9 copy-done.1
  3.0 22.5 %shard_map.162 = (f32[8,16,128]{2,1,0:T(8,128)S(1)}, bf16[8,64,1024]{2,1,0:T(8,128)(2,1)S(1)}) custom-call(f32[16,128]{1,0:T(8,128)S(1)} %select_maximum_fusion.refs_0_, bf16[64,1024]{1,0:T(8,128)(2,1)S(1)} %copy-done.1), custom_call_target="tpu_custom_call" | custom-call | bytes 44564480 | tf_op jit(solution)/shard_map/pallas_call | solution.py:134
  25.7 0.3 fusion.9
  26.0 0.3 iota_compare_fusion
  26.3 2.6 convolution_convert_fusion
  28.9 7.6 %all-to-all-start = ((bf16[16,64,1024]{2,1,0:T(8,128)(2,1)}), bf16[16,64,1024]{2,1,0:T(8,128)(2,1)S(1)}, u32[]{:S(2)}, u32[]{:S(2)}) async-start(bf16[16,64,1024]{2,1,0:T(8,128)(2,1)} %bitcast.138), calls=%async_computation | async-start | bytes 4194304 | tf_op jit(solution)/shard_map/all_to_all | solution.py:246
  36.7 0.3 select_reduce_fusion
  37.1 18.7 %shard_map.163 = bf16[8,64,1024]{2,1,0:T(8,128)(2,1)S(1)} custom-call(bf16[64,1024]{1,0:T(8,128)(2,1)S(1)} %copy-done), custom_call_target="tpu_custom_call" | custom-call | bytes 41943040 | tf_op jit(solution)/shard_map/pallas_call | solution.py:134
  55.8 2.6 multiply_convert_fusion
  58.4 2.2 all-to-all-done
  60.6 6.7 %all-to-all-start.1 = ((bf16[16,64,1024]{2,1,0:T(8,128)(2,1)}), bf16[16,64,1024]{2,1,0:T(8,128)(2,1)}, u32[]{:S(2)}, u32[]{:S(2)}) async-start(bf16[16,64,1024]{2,1,0:T(8,128)(2,1)} %bitcast.139), calls=%async_computation.1 | async-start | bytes 4194304 | tf_op jit(solution)/shard_map/all_to_all | solution.py:246
  67.4 5.0 %fusion.5 = f32[1024,768]{0,1:T(8,128)} fusion(bf16[1024,1024]{1,0:T(8,128)(2,1)S(1)} %bitcast.136, bf16[1,1024,768]{2,1,0:T(8,128)(2,1)} %param.15), kind=kOutput, calls=%fused_computation.15 | convolution fusion | flops 1610612736 | bytes 6815744 | tf_op jit(solution)/shard_map/dot_general | solution.py:276
  72.3 18.8 %all-to-all-done.1 = bf16[16,64,1024]{2,1,0:T(8,128)(2,1)} async-done(((bf16[16,64,1024]{2,1,0:T(8,128)(2,1)}), bf16[16,64,1024]{2,1,0:T(8,128)(2,1)}, u32[]{:S(2)}, u32[]{:S(2)}) %all-to-all-start.1) | async-done | bytes 2097184 | tf_op jit(solution)/shard_map/all_to_all | solution.py:246
  91.1 4.9 %multiply_convert_fusion.3 = (bf16[1024,384]{0,1:T(8,128)(2,1)S(1)}, bf16[1024,384]{0,1:T(8,128)(2,1)S(1)}, bf16[1024,384]{0,1:T(8,128)(2,1)}) fusion(f32[1024,768]{0,1:T(8,128)} %fusion.5, bf16[1024,1024]{1,0:T(8,128)(2,1)} %bitcast.13, bf16[1,384,1024]{2,1,0:T(8,128)(2,1)S(1)} %copy-done.9), kind=kOutput, calls=%fused_computation.23 | convolution fusion | flops 811204608 | bytes 8388608 | tf_op jit(solution)/shard_map/dot_general | solution.py:282
  96.0 1.3 pad_maximum_fusion
  97.2 0.7 copy-done.8
  98.0 1.8 convolution_convert_fusion.1
  99.8 1.6 copy.29
  101.4 12.5 %all-to-all-start.2 = ((bf16[128,8,1024]{2,1,0:T(8,128)(2,1)}), bf16[128,8,1024]{2,1,0:T(8,128)(2,1)S(1)}, u32[]{:S(2)}, u32[]{:S(2)}) async-start(bf16[128,8,1024]{2,1,0:T(8,128)(2,1)} %bitcast.132), calls=%async_computation.2 | async-start | bytes 4194304 | tf_op jit(solution)/shard_map/all_to_all | solution.py:232
  113.9 4.0 %fusion.44 = f32[1024,768]{1,0:T(8,128)S(1)} fusion(bf16[1024,1024]{1,0:T(8,128)(2,1)} %bitcast.137, bf16[1024,768]{0,1:T(8,128)(2,1)} %pad_maximum_fusion), kind=kOutput, calls=%fused_computation.103 | convolution fusion | flops 1610612736 | bytes 6815744 | tf_op jit(solution)/shard_map/dot_general | solution.py:298
  117.8 1.1 dynamic-slice_convert_fusion
  118.9 2.8 fusion.45
  121.8 0.9 dynamic-slice_convert_fusion.1
  122.6 0.4 copy-done.3
  123.0 0.3 collective-permute-start.1
  123.3 1.7 collective-permute-done.1
  125.0 1.8 abs_reduce_fusion.1
  126.8 2.1 abs_reduce_fusion
  130.2 3.0 pmax.7
  133.9 3.9 %fusion.23 = (bf16[512,768]{1,0:T(8,128)(2,1)S(1)}, bf16[512,768]{1,0:T(8,128)(2,1)S(1)}, bf16[512,768]{1,0:T(8,128)(2,1)S(1)}) fusion(f32[]{:T(128)S(6)} %div.36, f32[1,512,768]{2,1,0:T(8,128)} %param.18, bf16[512,768]{1,0:T(8,128)(2,1)S(1)} %collective-permute-done, f32[1024,768]{1,0:T(8,128)} %copy-done.2, s32[]{:T(128)S(6)} %select_n.84, ...), kind=kLoop, calls=%fused_computation.54 | loop fusion | flops 7864320 | bytes 8650760 | tf_op jit(solution)/shard_map/convert_element_type | solution.py:203
  137.9 0.9 constant_dynamic-update-slice_fusion.5
  138.8 0.9 constant_dynamic-update-slice_fusion.4
  139.8 1.0 constant_dynamic-update-slice_fusion.3
  140.7 0.7 fusion.29
  141.5 0.8 constant_dynamic-update-slice_fusion.2
  142.3 0.8 constant_dynamic-update-slice_fusion.1
  143.0 0.8 constant_dynamic-update-slice_fusion
  143.8 0.7 broadcast_dynamic-update-slice_fusion
  144.5 19.6 %all-to-all-done.2 = bf16[128,8,1024]{2,1,0:T(8,128)(2,1)S(1)} async-done(((bf16[128,8,1024]{2,1,0:T(8,128)(2,1)}), bf16[128,8,1024]{2,1,0:T(8,128)(2,1)S(1)}, u32[]{:S(2)}, u32[]{:S(2)}) %all-to-all-start.2) | async-done | bytes 2097184 | tf_op jit(solution)/shard_map/all_to_all | solution.py:232
  164.1 7.7 %all-to-all-start.3 = ((bf16[128,14,8,128]{3,2,1,0:T(8,128)(2,1)}), bf16[128,14,8,128]{3,2,1,0:T(8,128)(2,1)}, u32[]{:S(2)}, u32[]{:S(2)}) async-start(bf16[128,14,8,128]{3,2,1,0:T(8,128)(2,1)} %bitcast.40), calls=%async_computation.3 | async-start | bytes 7340032 | tf_op jit(solution)/shard_map/all_to_all | solution.py:329
  172.1 81.8 %all-to-all-done.3 = bf16[128,14,8,128]{3,2,1,0:T(8,128)(2,1)} async-done(((bf16[128,14,8,128]{3,2,1,0:T(8,128)(2,1)}), bf16[128,14,8,128]{3,2,1,0:T(8,128)(2,1)}, u32[]{:S(2)}, u32[]{:S(2)}) %all-to-all-start.3) | async-done | bytes 3670048 | tf_op jit(solution)/shard_map/all_to_all | solution.py:329
  253.9 4.9 %gather_fusion = bf16[128,14,8,128]{3,2,1,0:T(8,128)(2,1)} fusion(bf16[128,14,8,128]{3,2,1,0:T(8,128)(2,1)} %all-to-all-done.3, s32[1024]{0:T(1024)S(1)} %pad_clamp_fusion), kind=kCustom, calls=%fused_computation | custom fusion | bytes 7340544 | tf_op jit(solution)/shard_map/gather | solution.py:333
  258.8 8.8 %all-to-all-start.4 = ((bf16[128,14,8,128]{3,2,1,0:T(8,128)(2,1)}), bf16[128,14,8,128]{3,2,1,0:T(8,128)(2,1)}, u32[]{:S(2)}, u32[]{:S(2)}) async-start(bf16[128,14,8,128]{3,2,1,0:T(8,128)(2,1)} %gather_fusion), calls=%async_computation.4 | async-start | bytes 7340032 | tf_op jit(solution)/shard_map/all_to_all | solution.py:334
  268.2 1.3 convolution_convert_fusion.2
  269.5 80.1 %all-to-all-done.4 = bf16[128,14,8,128]{3,2,1,0:T(8,128)(2,1)} async-done(((bf16[128,14,8,128]{3,2,1,0:T(8,128)(2,1)}), bf16[128,14,8,128]{3,2,1,0:T(8,128)(2,1)}, u32[]{:S(2)}, u32[]{:S(2)}) %all-to-all-start.4) | async-done | bytes 3670048 | tf_op jit(solution)/shard_map/all_to_all | solution.py:334
  349.6 6.6 %shard_map.164 = (bf16[512,768]{1,0:T(8,128)(2,1)}, f32[512,768]{1,0:T(8,128)}, f32[512,768]{1,0:T(8,128)}, bf16[384,512]{1,0:T(8,128)(2,1)}, f32[384,512]{1,0:T(8,128)}, /*index=5*/f32[384,512]{1,0:T(8,128)}) custom-call(bf16[1792,8,128]{2,1,0:T(8,128)(2,1)} %bitcast.50.refs_0_.refs_1_.refs_2_.refs_3_.refs_4_.refs_5_, ...), custom_call_target="tpu_custom_call" | custom-call | tf_op jit(solution)/shard_map/pallas_call | solution.py:178
  (50 shorter events, 1.4 us)
Async XLA Ops:
  2.1 0.9 copy-start.1
  28.9 8.2 %copy-start = (bf16[64,1024]{1,0:T(8,128)(2,1)S(1)}, bf16[64,1024]{1,0:T(8,128)(2,1)}, u32[]{:S(2)}) copy-start(bf16[64,1024]{1,0:T(8,128)(2,1)} %refs_0_) | copy-start | bytes 393220
  28.9 31.7 %all-to-all-start = ((bf16[16,64,1024]{2,1,0:T(8,128)(2,1)}), bf16[16,64,1024]{2,1,0:T(8,128)(2,1)S(1)}, u32[]{:S(2)}, u32[]{:S(2)}) async-start(bf16[16,64,1024]{2,1,0:T(8,128)(2,1)} %bitcast.138), calls=%async_computation | async-start | bytes 4194304 | tf_op jit(solution)/shard_map/all_to_all | solution.py:246
  60.6 6.7 %copy-start.5 = (bf16[16,64,1024]{2,1,0:T(8,128)(2,1)}, bf16[16,64,1024]{2,1,0:T(8,128)(2,1)S(1)}, u32[]{:S(2)}) copy-start(bf16[16,64,1024]{2,1,0:T(8,128)(2,1)S(1)} %all-to-all-done) | copy-start | bytes 6291460
  60.6 30.4 %all-to-all-start.1 = ((bf16[16,64,1024]{2,1,0:T(8,128)(2,1)}), bf16[16,64,1024]{2,1,0:T(8,128)(2,1)}, u32[]{:S(2)}, u32[]{:S(2)}) async-start(bf16[16,64,1024]{2,1,0:T(8,128)(2,1)} %bitcast.139), calls=%async_computation.1 | async-start | bytes 4194304 | tf_op jit(solution)/shard_map/all_to_all | solution.py:246
  67.3 23.7 %copy-start.9 = (bf16[1,384,1024]{2,1,0:T(8,128)(2,1)S(1)}, bf16[1,384,1024]{2,1,0:T(8,128)(2,1)}, u32[]{:S(2)}) copy-start(bf16[1,384,1024]{2,1,0:T(8,128)(2,1)} %param.16) | copy-start | bytes 2359300
  96.0 2.0 copy-start.8
  101.4 62.7 %all-to-all-start.2 = ((bf16[128,8,1024]{2,1,0:T(8,128)(2,1)}), bf16[128,8,1024]{2,1,0:T(8,128)(2,1)S(1)}, u32[]{:S(2)}, u32[]{:S(2)}) async-start(bf16[128,8,1024]{2,1,0:T(8,128)(2,1)} %bitcast.132), calls=%async_computation.2 | async-start | bytes 4194304 | tf_op jit(solution)/shard_map/all_to_all | solution.py:232
  113.9 5.1 %copy-start.13 = (bf16[1024,384]{0,1:T(8,128)(2,1)S(1)}, bf16[1024,384]{0,1:T(8,128)(2,1)}, u32[]{:S(2)}) copy-start(bf16[1024,384]{0,1:T(8,128)(2,1)} %get-tuple-element.27) | copy-start | bytes 2359300
  117.8 3.9 %copy-start.2 = (f32[1024,768]{1,0:T(8,128)}, f32[1024,768]{1,0:T(8,128)S(1)}, u32[]{:S(2)}) copy-start(f32[1024,768]{1,0:T(8,128)S(1)} %fusion.44) | copy-start | bytes 9437188
  118.9 7.9 %collective-permute-start = (bf16[512,768]{1,0:T(8,128)(2,1)}, bf16[512,768]{1,0:T(8,128)(2,1)S(1)}, u32[]{:S(2)}, u32[]{:S(2)}) collective-permute-start(bf16[512,768]{1,0:T(8,128)(2,1)} %dynamic-slice_convert_fusion), channel_id=1, source_target_pairs={{0,128},{128,0},{1,129},{129,1},{2,130},{130,2},{3,131},{131,3},{4... | collective-permute-start | bytes 2359304 | tf_op jit(solution)/shard_map/ppermute | solution.py:307
  121.8 1.3 copy-start.3
  123.0 1.9 collective-permute-start.1
  137.9 2.9 copy-start.4
  137.9 2.9 copy-start.6
  137.9 2.9 copy-start.7
  137.9 2.8 copy-start.10
  164.1 7.8 %copy-start.12 = (s32[32,2]{0,1:T(2,128)S(1)}, s32[32,2]{0,1:T(2,128)}, u32[]{:S(2)}) copy-start(s32[32,2]{0,1:T(2,128)} %param.21) | copy-start | bytes 772
  164.1 89.8 %all-to-all-start.3 = ((bf16[128,14,8,128]{3,2,1,0:T(8,128)(2,1)}), bf16[128,14,8,128]{3,2,1,0:T(8,128)(2,1)}, u32[]{:S(2)}, u32[]{:S(2)}) async-start(bf16[128,14,8,128]{3,2,1,0:T(8,128)(2,1)} %bitcast.40), calls=%async_computation.3 | async-start | bytes 7340032 | tf_op jit(solution)/shard_map/all_to_all | solution.py:329
  258.8 8.8 %copy-start.11 = (s32[64,8]{0,1:T(8,128)S(1)}, s32[64,8]{0,1:T(8,128)}, u32[]{:S(2)}) copy-start(s32[64,8]{0,1:T(8,128)} %param.14) | copy-start | bytes 6148
  258.8 90.8 %all-to-all-start.4 = ((bf16[128,14,8,128]{3,2,1,0:T(8,128)(2,1)}), bf16[128,14,8,128]{3,2,1,0:T(8,128)(2,1)}, u32[]{:S(2)}, u32[]{:S(2)}) async-start(bf16[128,14,8,128]{3,2,1,0:T(8,128)(2,1)} %gather_fusion), calls=%async_computation.4 | async-start | bytes 7340032 | tf_op jit(solution)/shard_map/all_to_all | solution.py:334
